TPU v7x, 256 devices: a whole 4x4x8 slice. The times are simulated.
256 devices in a mesh: gx: 8 (over z), gy: 32 (over y, x, core).
Axes of the slice: x: 4, y: 4, z: 8, core: 2. Of those that a mesh axis runs over, the one named last changes fastest.
Arguments:
- child_coef: bfloat16 [512, 16, 128, 128], P(('gx', 'gy')), may hold values from -6 to 6
- transfer: bfloat16 [512, 64, 2, 128, 128], P(('gx', 'gy')), may hold values from -0.125 to 0.125
- child_dir: int32 [512, 64], P(('gx', 'gy')), may hold values from 0 to 15, as said below
- couple_src: int32 [64, 64, 7], P('gx', 'gy'), may hold values from 0 to 63, as said below
- couple_kind: int32 [64, 64, 7], P('gx', 'gy'), may hold values from 0 to 7
- couple_count: int32 [64, 64], P('gx', 'gy'), may hold values from 1 to 7, as said below
- couple_table: bfloat16 [64, 8, 2, 128, 128], P('gy'), may hold values from -0.1875 to 0.1875
Outputs:
- child_local: bfloat16 [512, 16, 128, 128], P(('gx', 'gy'))
Inputs may be any that keep to these rules, and one draw needn't show every extreme that they name: `child_dir`: in every row each child direction is named by exactly four parent directions. `couple_src`: the entries of one block row are distinct and never the row's own parent cluster. `couple_count`: some row holds 7.
All inputs are finite; a program needn't handle non-finite values.
Results may differ from a plain program's by a relative error of at most 0.015.
Values may be sent and summed in bfloat16 or wider, within the bound.
A program may use at most 128 MiB of HBM per device.

v0:
```python
import jax
import jax.numpy as jnp
from jax import lax
from jax.sharding import PartitionSpec as P

CPD = 2


def complex_apply(real_part, imag_part, vectors, pattern):
    halfway = vectors.shape[-1] // 2
    real_term = jnp.einsum(pattern, real_part, vectors, preferred_element_type=jnp.float32)
    imag_term = jnp.einsum(pattern, imag_part, vectors, preferred_element_type=jnp.float32)
    return jnp.concatenate(
        [
            real_term[..., :halfway] - imag_term[..., halfway:],
            real_term[..., halfway:] + imag_term[..., :halfway],
        ],
        axis=-1,
    )


def sum_groups(received):
    groups = received.shape[0] // (8 // CPD)
    merged = received.astype(jnp.float32).reshape((groups, 8 // CPD) + received.shape[1:])
    return jnp.sum(merged, axis=1).astype(jnp.bfloat16)


def body(child_coef, transfer, child_dir, couple_src, couple_kind, couple_count, couple_table):
    picked = jnp.take_along_axis(child_coef, child_dir[:, :, None, None], axis=1)
    upward = complex_apply(transfer[:, :, 0], transfer[:, :, 1], picked, "cers,cesa->cera")
    summed = jnp.sum(upward, axis=0, keepdims=True).astype(jnp.bfloat16)
    parent = sum_groups(lax.all_to_all(summed, "gy", split_axis=1, concat_axis=0, tiled=True))
    everything = lax.all_gather(parent, "gx", axis=0, tiled=True)
    dir_local = jnp.arange(parent.shape[1], dtype=jnp.int32)[None, :, None]
    sources = everything[couple_src, dir_local]
    matrices = couple_table[dir_local, couple_kind]
    products = complex_apply(
        matrices[:, :, :, 0], matrices[:, :, :, 1], sources, "uemrs,uemsa->uemra"
    )
    active = jnp.arange(couple_src.shape[-1], dtype=jnp.int32) < couple_count[..., None]
    parent_local = jnp.sum(jnp.where(active[..., None, None], products, 0.0), axis=2).astype(
        jnp.bfloat16
    )
    copies = jnp.repeat(parent_local, 8 // CPD, axis=0)
    parent_row = lax.all_to_all(copies, "gy", split_axis=0, concat_axis=1, tiled=True)[0]
    descent = complex_apply(transfer[:, :, 0], transfer[:, :, 1], parent_row, "cesr,esa->cera")
    child_index = jnp.arange(child_coef.shape[1], dtype=jnp.int32)
    onehot = (child_dir[:, None, :] == child_index[None, :, None]).astype(jnp.float32)
    child_local = jnp.einsum("cie,cera->cira", onehot, descent)
    return child_local.astype(jnp.bfloat16)


def solution(mesh):
    return jax.shard_map(
        body,
        mesh=mesh,
        in_specs=(
            P(("gx", "gy"), None, None, None),
            P(("gx", "gy"), None, None, None, None),
            P(("gx", "gy"), None),
            P("gx", "gy", None),
            P("gx", "gy", None),
            P("gx", "gy"),
            P("gy", None, None, None, None),
        ),
        out_specs=P(("gx", "gy"), None, None, None),
        check_vma=False,
    )
```

profile of v0, /device:TPU:1, one launch (start us, length us, event | category | flops | bytes accessed | tf_op | source)
XLA Modules:
  0.0 241.7 jit_solution(4865288829287410528)
XLA Ops:
  6.5 0.0 copy-start
  6.5 0.0 all-gather.2.cloned.1.call-start
  6.5 0.8 bitcast_or_fusion
  7.3 0.7 compare_and_fusion
  8.0 0.1 reshape.63
  8.1 4.3 %gather_fusion.2 = bf16[128,128,128]{2,1,0:T(8,128)(2,1)} fusion(bf16[2,16,128,128]{3,2,1,0:T(8,128)(2,1)} %param.7, s32[128]{0:T(128)S(1)} %reshape.63), kind=kCustom, calls=%fused_computation.2 | custom fusion | bytes 8389632 | tf_op jit(solution)/shard_map/jit(take_along_axis)/gather | solution.py:29
  12.4 6.3 %copy.35 = bf16[2,64,128,128]{2,3,1,0:T(8,128)(2,1)} copy(bf16[2,64,128,128]{3,2,1,0:T(8,128)(2,1)} %bitcast.69) | data formatting | bytes 8388608 | tf_op jit(solution)/shard_map/jit(take_along_axis)/gather | solution.py:29
  18.7 0.0 copy-start.2
  18.7 9.9 %fusion.10 = f32[2,64,128,128]{2,3,1,0:T(8,128)} fusion(bf16[2,64,128,128]{2,3,1,0:T(8,128)(2,1)} %copy.35, pred[2,64]{1,0:T(4,128)(4,1)S(1)} %compare_and_fusion, bf16[2,64,2,128,128]{4,3,2,1,0:T(8,128)(2,1)} %param.8), kind=kOutput, calls=%fused_computation.27 | convolution fusion | flops 538968064 | bytes 16777344 | tf_op jit(solution)/shard_map/cers,cesa->cera/dot_general | solution.py:12
  28.6 0.0 copy-done.2
  28.6 8.5 %fusion.9 = f32[2,64,128,128]{2,3,1,0:T(8,128)} fusion(bf16[2,64,128,128]{2,3,1,0:T(8,128)(2,1)S(1)} %copy-done.2, pred[2,64]{1,0:T(4,128)(4,1)S(1)} %compare_and_fusion, bf16[2,64,2,128,128]{4,3,2,1,0:T(8,128)(2,1)} %param.8), kind=kOutput, calls=%fused_computation.26 | convolution fusion | flops 538968064 | bytes 16777344 | tf_op jit(solution)/shard_map/cers,cesa->cera/dot_general | solution.py:11
  37.1 10.3 %slice_subtract_fusion.1 = (f32[2,64,128,64]{2,3,1,0:T(8,128)S(1)}, f32[2,64,128,64]{2,3,1,0:T(8,128)}) fusion(f32[2,64,128,128]{2,3,1,0:T(8,128)} %fusion.10, f32[2,64,128,128]{2,3,1,0:T(8,128)} %fusion.9), kind=kLoop, calls=%fused_computation.10 | loop fusion | flops 2097152 | bytes 25165824 | tf_op jit(solution)/shard_map/sub | solution.py:15
  47.5 5.0 %maximum_reduce_fusion = bf16[64,128,128]{1,2,0:T(8,128)(2,1)} fusion(f32[2,64,128,64]{2,3,1,0:T(8,128)} %get-tuple-element.8, f32[2,64,128,64]{2,3,1,0:T(8,128)S(1)} %get-tuple-element.7), kind=kLoop, calls=%fused_computation.3 | loop fusion | flops 3145728 | bytes 10485760 | tf_op jit(solution)/shard_map/reduce_sum | solution.py:31
  52.4 4.1 %copy.38 = bf16[1,64,128,128]{3,2,0,1:T(8,128)(2,1)} copy(bf16[1,64,128,128]{2,3,1,0:T(8,128)(2,1)} %bitcast.70) | data formatting | bytes 4194304 | tf_op jit(solution)/shard_map/convert_element_type | solution.py:31
  56.5 0.0 copy-start.7
  56.5 0.0 copy-start.8
  56.5 37.0 %all_to_all.21 = bf16[1,64,128,128]{3,2,0,1:T(8,128)(2,1)S(1)} all-to-all(bf16[1,64,128,128]{3,2,0,1:T(8,128)(2,1)} %copy.38), channel_id=1, replica_groups=mesh['gx'=8,'gy'=32] {'gy'}, dimensions={1} | all-to-all | bytes 4194304 | tf_op jit(solution)/shard_map/all_to_all | solution.py:32
  93.5 1.3 reduce_sum.31
  94.8 0.0 all-gather.2.cloned.1.call-update
  94.8 0.0 copy-done.7
  94.9 0.1 copy.39
  94.9 0.1 reshape.57
  95.0 0.0 copy-done.8
  95.1 0.1 copy.33
  95.2 0.1 reshape.51
  95.3 0.0 copy-done
  95.3 7.8 %gather_fusion = bf16[112,2,128,128]{3,2,1,0:T(8,128)(2,1)} fusion(bf16[2,8,2,128,128]{4,3,2,1,0:T(8,128)(2,1)S(1)} %copy-done, s32[112]{0:T(128)S(1)} %reshape.51), kind=kCustom, calls=%fused_computation | custom fusion | bytes 14680960 | tf_op jit(solution)/shard_map/gather | solution.py:36
  103.1 0.0 copy-start.9
  103.1 9.4 %copy.34 = bf16[112,2,128,128]{3,2,0,1:T(8,128)(2,1)} copy(bf16[112,2,128,128]{3,2,1,0:T(8,128)(2,1)} %gather_fusion) | data formatting | bytes 14680064 | tf_op jit(solution)/shard_map/gather | solution.py:36
  112.5 0.0 copy-done.9
  112.5 0.1 copy.32
  112.5 0.1 iota_compare_fusion.1
  112.6 36.0 %all-gather.2.cloned.1.call-done = bf16[64,2,128,128]{3,2,1,0:T(8,128)(2,1)} async-done(((bf16[8,2,128,128]{3,2,1,0:T(8,128)(2,1)}), bf16[64,2,128,128]{3,2,1,0:T(8,128)(2,1)}) %all-gather.2.cloned.1.call-update) | async-done | bytes 4194320 | tf_op jit(solution)/shard_map/all_gather | solution.py:33
  148.6 5.5 %gather_fusion.1 = bf16[112,128,128]{2,1,0:T(8,128)(2,1)} fusion(bf16[64,2,128,128]{3,2,1,0:T(8,128)(2,1)} %all-gather.2.cloned.1.call-done, s32[112]{0:T(128)S(1)} %reshape.57), kind=kCustom, calls=%fused_computation.1 | custom fusion | bytes 7340928 | tf_op jit(solution)/shard_map/gather | solution.py:35
  154.1 0.0 copy-start.3
  154.1 0.0 copy-start.4
  154.1 6.0 %fusion.7 = f32[8,2,7,128,128]{3,4,2,1,0:T(8,128)S(1)} fusion(bf16[8,2,7,128,128]{4,3,2,1,0:T(8,128)(2,1)} %bitcast.63, bf16[8,2,7,2,128,128]{5,4,2,1,0,3:T(8,128)(2,1)} %bitcast.65), kind=kOutput, calls=%fused_computation.23 | convolution fusion | flops 469762048 | bytes 14680064 | tf_op jit(solution)/shard_map/uemrs,uemsa->uemra/dot_general | solution.py:12
  160.1 0.0 copy-done.3
  160.1 0.3 copy-done.4
  160.5 5.6 %fusion.8 = f32[8,2,7,128,128]{3,4,2,1,0:T(8,128)} fusion(bf16[8,2,7,128,128]{4,3,2,1,0:T(8,128)(2,1)S(1)} %bitcast.64, bf16[8,2,7,2,128,128]{5,4,2,1,0,3:T(8,128)(2,1)S(1)} %bitcast.66), kind=kOutput, calls=%fused_computation.25 | convolution fusion | flops 469762048 | bytes 14680064 | tf_op jit(solution)/shard_map/uemrs,uemsa->uemra/dot_general | solution.py:11
  166.1 7.7 %slice_subtract_fusion.2 = (f32[8,2,7,128,64]{3,4,2,1,0:T(8,128)S(1)}, f32[8,2,7,128,64]{3,4,2,1,0:T(8,128)}) fusion(f32[8,2,7,128,128]{3,4,2,1,0:T(8,128)S(1)} %fusion.7, f32[8,2,7,128,128]{3,4,2,1,0:T(8,128)} %fusion.8), kind=kLoop, calls=%fused_computation.21 | loop fusion | flops 1835008 | bytes 22020096 | tf_op jit(solution)/shard_map/sub | solution.py:15
  173.8 2.8 %fusion = bf16[8,2,128,128]{2,3,1,0:T(8,128)(2,1)S(1)} fusion(f32[8,2,7,128,64]{3,4,2,1,0:T(8,128)} %get-tuple-element.10, f32[8,2,7,128,64]{3,4,2,1,0:T(8,128)S(1)} %get-tuple-element.9, pred[8,2,7]{2,1,0:T(4,128)(4,1)S(1)} %iota_compare_fusion.1), kind=kLoop, calls=%fused_computation.6 | loop fusion | flops 5242880 | bytes 7864432 | tf_op jit(solution)/shard_map/reduce_sum | solution.py:41
  176.6 1.9 broadcast_in_dim.55
  178.5 7.7 %all-to-all-start.1 = ((bf16[32,2,128,128]{2,3,1,0:T(8,128)(2,1)}), bf16[32,2,128,128]{2,3,1,0:T(8,128)(2,1)S(1)}, u32[]{:S(2)}, u32[]{:S(2)}) async-start(bf16[32,2,128,128]{2,3,1,0:T(8,128)(2,1)} %bitcast.71), calls=%async_computation.1 | async-start | bytes 4194304 | tf_op jit(solution)/shard_map/all_to_all | solution.py:45
  186.2 6.1 %slice_bitcast_fusion.1 = (bf16[2,64,128,128]{3,2,1,0:T(8,128)(2,1)}, bf16[2,64,128,128]{3,2,1,0:T(8,128)(2,1)}) fusion(bf16[2,64,2,128,128]{4,3,2,1,0:T(8,128)(2,1)} %param.8), kind=kLoop, calls=%fused_computation.16 | loop fusion | bytes 16777216 | tf_op jit(solution)/shard_map/squeeze | solution.py:30
  192.3 22.5 %all-to-all-done.1 = bf16[32,2,128,128]{2,3,1,0:T(8,128)(2,1)S(1)} async-done(((bf16[32,2,128,128]{2,3,1,0:T(8,128)(2,1)}), bf16[32,2,128,128]{2,3,1,0:T(8,128)(2,1)S(1)}, u32[]{:S(2)}, u32[]{:S(2)}) %all-to-all-start.1) | async-done | bytes 2097184 | tf_op jit(solution)/shard_map/all_to_all | solution.py:45
  214.8 0.0 copy-start.5
  214.8 3.6 %fusion.11 = f32[2,64,128,128]{2,3,0,1:T(8,128)S(1)} fusion(bf16[64,128,128,1]{1,2,3,0:T(8,128)(2,1)S(1)} %bitcast.67, bf16[2,64,128,128]{3,2,1,0:T(8,128)(2,1)} %get-tuple-element.11), kind=kOutput, calls=%fused_computation.28 | convolution fusion | flops 536870912 | bytes 14680064 | tf_op jit(solution)/shard_map/cesr,esa->cera/dot_general | solution.py:11
  218.4 0.0 copy-done.5
  218.4 1.2 fusion.14
  219.7 2.1 slice_subtract_fusion
  221.8 2.3 pad_maximum_fusion
  224.0 0.0 copy-start.6
  224.0 0.0 copy-start.1
  224.0 6.7 %copy.44 = bf16[2,64,128,128]{3,1,2,0:T(8,128)(2,1)} copy(bf16[2,64,128,128]{2,3,0,1:T(8,128)(2,1)} %pad_maximum_fusion) | data formatting | bytes 8388608 | tf_op jit(solution)/shard_map/concatenate | solution.py:13
  230.7 0.0 copy-done.6
  230.7 2.8 %convolution_convert_fusion = bf16[2,16,128,128]{3,1,2,0:T(8,128)(2,1)S(1)} fusion(bf16[2,64,128,128]{3,1,2,0:T(8,128)(2,1)} %copy.44, s32[2,64]{1,0:T(2,128)S(1)} %copy-done.6), kind=kOutput, calls=%fused_computation.33 | convolution fusion | flops 67110912 | bytes 5243392 | tf_op jit(solution)/shard_map/cie,cera->cira/dot_general | solution.py:49
  233.6 1.2 copy.45
  234.8 0.0 copy-done.1
  (2 shorter events, 0.0 us)
Async XLA Ops:
  6.5 88.7 %copy-start = (bf16[2,8,2,128,128]{4,3,2,1,0:T(8,128)(2,1)S(1)}, bf16[2,8,2,128,128]{4,3,2,1,0:T(8,128)(2,1)}, u32[]{:S(2)}) copy-start(bf16[2,8,2,128,128]{4,3,2,1,0:T(8,128)(2,1)} %param.13) | copy-start | bytes 3145732
  6.5 142.1 %all-gather.2.cloned.1.call-start = ((), (), s32[]{:S(2)}) async-start(), calls=%async_computation.2 | async-start | bytes 4718592 | tf_op jit(solution)/shard_map/all_gather | solution.py:33
  18.7 9.9 %copy-start.2 = (bf16[2,64,128,128]{2,3,1,0:T(8,128)(2,1)S(1)}, bf16[2,64,128,128]{2,3,1,0:T(8,128)(2,1)}, u32[]{:S(2)}) copy-start(bf16[2,64,128,128]{2,3,1,0:T(8,128)(2,1)} %copy.35) | copy-start | bytes 12582916
  56.5 38.3 %copy-start.7 = (s32[8,2,7]{0,1,2:T(2,128)S(1)}, s32[8,2,7]{0,1,2:T(2,128)}, u32[]{:S(2)}) copy-start(s32[8,2,7]{0,1,2:T(2,128)} %param.10) | copy-start | bytes 1348
  56.5 38.6 %copy-start.8 = (s32[8,2,7]{0,1,2:T(2,128)S(1)}, s32[8,2,7]{0,1,2:T(2,128)}, u32[]{:S(2)}) copy-start(s32[8,2,7]{0,1,2:T(2,128)} %param.11) | copy-start | bytes 1348
  103.1 9.4 %copy-start.9 = (s32[8,2]{0,1:T(2,128)S(1)}, s32[8,2]{0,1:T(2,128)}, u32[]{:S(2)}) copy-start(s32[8,2]{0,1:T(2,128)} %param.12) | copy-start | bytes 196
  154.1 6.0 %copy-start.3 = (bf16[112,128,128]{2,1,0:T(8,128)(2,1)S(1)}, bf16[112,128,128]{2,1,0:T(8,128)(2,1)}, u32[]{:S(2)}) copy-start(bf16[112,128,128]{2,1,0:T(8,128)(2,1)} %gather_fusion.1) | copy-start | bytes 11010052
  154.1 6.3 %copy-start.4 = (bf16[112,2,128,128]{3,2,0,1:T(8,128)(2,1)S(1)}, bf16[112,2,128,128]{3,2,0,1:T(8,128)(2,1)}, u32[]{:S(2)}) copy-start(bf16[112,2,128,128]{3,2,0,1:T(8,128)(2,1)} %copy.34) | copy-start | bytes 22020100
  178.5 36.3 %all-to-all-start.1 = ((bf16[32,2,128,128]{2,3,1,0:T(8,128)(2,1)}), bf16[32,2,128,128]{2,3,1,0:T(8,128)(2,1)S(1)}, u32[]{:S(2)}, u32[]{:S(2)}) async-start(bf16[32,2,128,128]{2,3,1,0:T(8,128)(2,1)} %bitcast.71), calls=%async_computation.1 | async-start | bytes 4194304 | tf_op jit(solution)/shard_map/all_to_all | solution.py:45
  214.8 3.6 %copy-start.5 = (bf16[2,64,128,128]{3,2,1,0:T(8,128)(2,1)S(1)}, bf16[2,64,128,128]{3,2,1,0:T(8,128)(2,1)}, u32[]{:S(2)}) copy-start(bf16[2,64,128,128]{3,2,1,0:T(8,128)(2,1)} %get-tuple-element.12) | copy-start | bytes 12582916
  224.0 6.7 %copy-start.6 = (s32[2,64]{1,0:T(2,128)S(1)}, s32[2,64]{1,0:T(2,128)}, u32[]{:S(2)}) copy-start(s32[2,64]{1,0:T(2,128)} %param.9) | copy-start | bytes 1540
  224.0 10.8 %copy-start.1 = (bf16[2,8,2,128,128]{4,3,2,1,0:T(8,128)(2,1)S(1)}, bf16[2,8,2,128,128]{4,3,2,1,0:T(8,128)(2,1)}, u32[]{:S(2)}) copy-start(bf16[2,8,2,128,128]{4,3,2,1,0:T(8,128)(2,1)} %param.13) | copy-start | bytes 3145732
Sparse Core Ops, SparseCore 0:
  94.9 53.6 all-gather.1
where the time goes:
time: 242 us
  waiting for transfers between devices  58.5 us (24%)
  local copies, waits for them, and re-layouts  54.1 us (22%)
  matrix products  37.7 us (16%)
  blocking collectives  37 us (15%)
  other arithmetic  33 us (14%)
  between operations  13.5 us (6%)
  starting transfers between devices  7.7 us (3%)
    all_to_all x1, blocking collectives, body(): lax.all_to_all(summed, 'gy', split_axis=1, concat_axis=0, tiled=True)  37 us
    all_gather x1, waiting for transfers between devices, body(): everything = lax.all_gather(parent, 'gx', axis=0, tiled=True)  36 us
    all_to_all x1, waiting for transfers between devices, body(): lax.all_to_all(copies, 'gy', split_axis=0, concat_axis=1, tiled=True)[0]  22.5 us
    sub x3, other arithmetic, complex_apply(): real_term[..., :halfway] - imag_term[..., halfway:]  20.1 us
    dot_general x3, matrix products, complex_apply(): jnp.einsum(pattern, real_part, vectors, preferred_element_type=jnp.float32)  17.7 us
    gather x2, local copies, waits for them, and re-layouts, body(): matrices = couple_table[dir_local, couple_kind]  17.2 us
    dot_general x3, matrix products, complex_apply(): jnp.einsum(pattern, imag_part, vectors, preferred_element_type=jnp.float32)  17.2 us
    gather x3, local copies, waits for them, and re-layouts, body(): jnp.take_along_axis(child_coef, child_dir[:, :, None, None], axis=1)  10.7 us
  transfers between devices with their start and end apart: 2, of which 2 were waited for; matrix products, arithmetic and copies ran while one was open for 10% of the time, Pallas kernels for 0%

commit v1 on v0

v1 whole, which is shorter than its diff:
```python
import functools

import jax
import jax.numpy as jnp
from jax import lax
from jax.experimental import pallas as pl
from jax.experimental.pallas import tpu as pltpu
from jax.sharding import PartitionSpec as P

MESH = pl.DeviceIdType.MESH
NT = (((1,), (1,)), ((), ()))
BF = jnp.bfloat16
F32 = jnp.float32
ZERO_SLOT = 512


def combine(z):
    z = z.reshape(z.shape[0] // 16, 2, 8, 256)
    re, im = z[:, 0], z[:, 1]
    out_re = re[:, :, :128] - im[:, :, 128:]
    out_im = im[:, :, :128] + re[:, :, 128:]
    return jnp.concatenate([out_re[:, None], out_im[:, None]], axis=1)


def kernel(
    dir_s, dir_v, idx_v, coef, table, tr_hbm,
    out,
    tr, vc, send_own, recv_c, tx, recv_x, fw, ry_m, ry_o, rz, pz, zk, lo, qz, fd, plo,
    idx_all, idx_s, list_v, list_s,
    sem_ld, sem_sm,
    cs, cr, xs, xr, fs, fr, ys, yr, zs, zr, is_, ir,
    zbs, zbr, ybs, ybr, fbs, fbr, xbs, xbr, cbs, cbr,
):
    z = lax.axis_index("gx")
    g = lax.axis_index("gy")
    c = lax.rem(g, 2)
    x = lax.rem(lax.div(g, 2), 4)
    y = lax.div(g, 8)
    xp = x + 1 - 2 * lax.rem(x, 2)
    xn = 3 - x
    xf = 3 - xp
    xh = lax.div(x, 2)
    oc = 1 - c

    def gid(yy, xx, cc):
        return (yy * 4 + xx) * 2 + cc

    dev_core = (z, gid(y, x, oc))
    dev_xp = (z, gid(y, xp, c))
    dev_xn = (z, gid(y, xn, c))

    def yo(dy):
        return lax.rem(y + dy, 4)

    def zo(dz):
        return lax.rem(z + dz, 8)

    def dev_y(yy):
        return (z, gid(yy, x, c))

    def dev_z(zz):
        return (zz, g)

    def rc(src, dst, ss, rs, dev):
        return pltpu.make_async_remote_copy(
            src_ref=src, dst_ref=dst, send_sem=ss, recv_sem=rs, device_id=dev, device_id_type=MESH
        )

    pend = []

    def go(cp):
        cp.start()
        pend.append(cp)

    YS = (2, 1, 3)
    ZS = (4, 3, 5, 2, 6, 1, 7)
    pri = (xf, xp, xn, x)

    barrier = pltpu.get_barrier_semaphore()
    partners = [dev_core, dev_xp, dev_xn] + [dev_y(yo(dy)) for dy in YS] + [dev_z(zo(dz)) for dz in ZS]
    for dev in partners:
        pl.semaphore_signal(barrier, inc=1, device_id=dev, device_id_type=MESH)

    loads = []
    for k in range(4):
        cp = pltpu.make_async_copy(tr_hbm.at[:, :, pri[k]], tr.at[:, :, pri[k]], sem_ld.at[k])
        cp.start()
        loads.append(cp)

    def prep(n, carry):
        cc = lax.div(n, 16)
        i = lax.rem(n, 16)
        vt = coef[cc, i].astype(F32).T.reshape(2, 8, 8, 128)
        v = jnp.concatenate([vt[0][:, None], vt[1][:, None]], axis=1)
        vc[cc, i] = v.reshape(128, 128).astype(BF)
        return carry

    lax.fori_loop(0, 32, prep, 0, unroll=2)

    pl.semaphore_wait(barrier, len(partners))

    for dz in ZS:
        go(rc(idx_v, idx_all.at[z], is_.at[zo(dz)], ir.at[z], dev_z(zo(dz))))
    idx_all[z] = idx_v[...]

    def up(d, k):
        def one(n, carry):
            yy = lax.rem(n, 4)
            first = lax.div(n, 4)
            cc = lax.rem(oc + first, 2)
            cd = cc * 2 + d
            e = yy * 16 + pri[k] * 4 + cd
            lhs = jnp.concatenate([vc[0, dir_s[0, e]], vc[1, dir_s[0, 64 + e]]], axis=1)
            rhs = jnp.concatenate(
                [tr[0, yy, pri[k], cd].reshape(256, 128), tr[1, yy, pri[k], cd].reshape(256, 128)], axis=1
            )
            r = combine(lax.dot_general(lhs, rhs, NT, preferred_element_type=F32))
            send_own[d, k, first, yy] = r.reshape(8, 16, 128).astype(BF)
            return carry

        lax.fori_loop(0, 8, one, 0, unroll=2)


    def core_send(d, k):
        go(rc(send_own.at[d, k, 0], recv_c.at[d, k], cs.at[d, k], cr.at[d, k], dev_core))

    def core_wait(d, k):
        rc(send_own.at[d, k, 0], recv_c.at[d, k], cs.at[d, k], cr.at[d, k], dev_core).wait_recv()

    def t_step(d, k):
        core_wait(d, k)
        for yy in range(4):
            tx[d, k, yy] = (send_own[d, k, 1, yy].astype(F32) + recv_c[d, k, yy].astype(F32)).astype(BF)
        go(rc(tx.at[d, k], recv_x.at[d, k], xs.at[d, k], xr.at[d, k], dev_xp))

    def x_wait(d, k):
        rc(tx.at[d, k], recv_x.at[d, k], xs.at[d, k], xr.at[d, k], dev_xp).wait_recv()

    def add3(d, k, yy):
        return (
            send_own[d, k + 2, 1, yy].astype(F32)
            + recv_c[d, k + 2, yy].astype(F32)
            + recv_x[d, k, yy].astype(F32)
        ).astype(BF)

    def f_step(d):
        core_wait(d, 2)
        x_wait(d, 0)
        for yy in range(4):
            fw[d, yy] = add3(d, 0, yy)
        go(rc(fw.at[d], ry_o.at[d], fs.at[d], fr.at[d], dev_xn))

    def y_copy(d, kind, src, yy):
        p = y * 2 + (xh if kind == 0 else 1 - xh)
        return rc(src.at[d, yy], rz.at[d, p], ys.at[d, kind, yy], yr.at[d, kind, y], dev_y(yy))

    def g_step(d):
        core_wait(d, 3)
        x_wait(d, 1)
        for yy in range(4):
            ry_m[d, yy] = add3(d, 1, yy)
        for dy in YS:
            go(y_copy(d, 0, ry_m, yo(dy)))
        rz[d, y * 2 + xh] = ry_m[d, y]

    def h_step(d):
        rc(fw.at[d], ry_o.at[d], fs.at[d], fr.at[d], dev_xn).wait_recv()
        for dy in YS:
            go(y_copy(d, 1, ry_o, yo(dy)))
        rz[d, y * 2 + 1 - xh] = ry_o[d, y]

    def z_send(d):
        for kind in range(2):
            for dy in YS:
                yy = yo(dy)
                p = yy * 2 + (xh if kind == 0 else 1 - xh)
                rc(ry_m.at[d, yy], rz.at[d, p], ys.at[d, kind, yy], yr.at[d, kind, yy], dev_y(yy)).wait_recv()
        for dz in ZS:
            zz = zo(dz)
            go(rc(rz.at[d, :, zz], pz.at[d, z], zs.at[d, zz], zr.at[d, z], dev_z(zz)))
        pz[d, z] = rz[d, :, z]

    order = [(d, k) for d in range(2) for k in range(4)]
    for n, (d, k) in enumerate(order):
        if d == 0:
            loads[k].wait()
        up(d, k)
        core_send(d, k)
        if n >= 1:
            pd, pk = order[n - 1]
            if pk < 2:
                t_step(pd, pk)

    row = jnp.broadcast_to(dir_v[...], (128, 128))
    lane = lax.broadcasted_iota(jnp.int32, (128, 128), 1)
    sub = lax.broadcasted_iota(jnp.int32, (128, 128), 0)
    row = row + jnp.where(lane >= 64, 16, 0)
    same = jnp.where((row == row.T) & (sub < lane), 1, 0)
    key = row * 4 + jnp.broadcast_to(jnp.sum(same, axis=0, keepdims=True), (128, 128))
    lst = jnp.sum(jnp.where(key.T == lane, sub, 0), axis=0, keepdims=True)
    list_v[...] = jnp.broadcast_to(lst, (8, 128))
    zk[ZERO_SLOT] = jnp.zeros((16, 128), F32)

    f_step(0)
    cp_list = pltpu.make_async_copy(list_v, list_s, sem_sm.at[0])
    cp_list.start()
    g_step(0)
    h_step(0)
    f_step(1)
    z_send(0)
    g_step(1)
    h_step(1)
    cp_list.wait()
    for dz in ZS:
        zz = zo(dz)
        rc(idx_v, idx_all.at[zz], is_.at[zz], ir.at[zz], dev_z(zz)).wait_recv()
    cp_idx = pltpu.make_async_copy(idx_all, idx_s, sem_sm.at[1])
    cp_idx.start()
    z_send(1)
    cp_idx.wait()

    def couple(d):
        for dz in ZS:
            zz = zo(dz)
            rc(rz.at[d, :, zz], pz.at[d, zz], zs.at[d, zz], zr.at[d, zz], dev_z(zz)).wait_recv()

        def dense(n, carry):
            k = lax.div(n, 4)
            q = lax.rem(n, 4)
            lhs = pz[d, pl.ds(q * 2, 2)].reshape(256, 128)
            r = combine(
                lax.dot_general(lhs, table[d, k].reshape(256, 128), NT, preferred_element_type=F32)
            )
            zk[pl.ds(n * 16, 16)] = r.reshape(16, 16, 128)
            return carry

        lax.fori_loop(0, 32, dense, 0)
        for dz in ZS + (0,):
            zz = zo(dz)

            def row_sum(p, carry):
                acc = zk[idx_s[zz, p, d * 8]]
                for m in range(1, 7):
                    acc = acc + zk[idx_s[zz, p, d * 8 + m]]
                lo[d, zz, p] = acc.astype(BF)
                return carry

            lax.fori_loop(0, 8, row_sum, 0, unroll=2)
            if dz:
                go(rc(lo.at[d, zz], qz.at[d, :, z], zbs.at[d, zz], zbr.at[d, z], dev_z(zz)))
        qz[d, :, z] = lo[d, z]

    def yb_step(d):
        for dz in ZS:
            zz = zo(dz)
            rc(lo.at[d, zz], qz.at[d, :, zz], zbs.at[d, zz], zbr.at[d, zz], dev_z(zz)).wait_recv()
        for dy in YS:
            yy = yo(dy)
            go(rc(qz.at[d, yy * 2 + 1 - xh], fd.at[d, y], ybs.at[d, 1, yy], ybr.at[d, 1, y], dev_y(yy)))
        for dy in YS:
            yy = yo(dy)
            go(rc(qz.at[d, yy * 2 + xh], plo.at[y, x, c * 2 + d], ybs.at[d, 0, yy], ybr.at[d, 0, y], dev_y(yy)))
        fd[d, y] = qz[d, y * 2 + 1 - xh]
        plo[y, x, c * 2 + d] = qz[d, y * 2 + xh]

    def grp(xx, cc, d):
        return plo.at[:, xx, cc * 2 + d]

    def cb_send(d, n, xx):
        go(rc(grp(xx, c, d), grp(xx, c, d), cbs.at[d, n], cbr.at[d, n], dev_core))

    cb_groups = (x, xn, xp, xf)

    def xb_step(d):
        for dy in YS:
            yy = yo(dy)
            rc(qz.at[d, yy * 2 + 1 - xh], fd.at[d, yy], ybs.at[d, 1, yy], ybr.at[d, 1, yy], dev_y(yy)).wait_recv()
        go(rc(fd.at[d], grp(x, c, d), fbs.at[d], fbr.at[d], dev_xn))
        for dy in YS:
            yy = yo(dy)
            rc(qz.at[d, yy * 2 + xh], plo.at[yy, x, c * 2 + d], ybs.at[d, 0, yy], ybr.at[d, 0, yy], dev_y(yy)).wait_recv()
        go(rc(grp(x, c, d), grp(x, c, d), xbs.at[d, 0], xbr.at[d, 0], dev_xp))
        cb_send(d, 0, x)

    def xb2_step(d):
        rc(fd.at[d], grp(xn, c, d), fbs.at[d], fbr.at[d], dev_xn).wait_recv()
        go(rc(grp(xn, c, d), grp(xn, c, d), xbs.at[d, 1], xbr.at[d, 1], dev_xp))
        cb_send(d, 1, xn)

    def xb3_step(d):
        rc(grp(x, c, d), grp(xp, c, d), xbs.at[d, 0], xbr.at[d, 0], dev_xp).wait_recv()
        cb_send(d, 2, xp)
        rc(grp(xn, c, d), grp(xf, c, d), xbs.at[d, 1], xbr.at[d, 1], dev_xp).wait_recv()
        cb_send(d, 3, xf)

    couple(0)
    couple(1)
    yb_step(0)
    xb_step(0)
    yb_step(1)
    xb2_step(0)
    xb3_step(0)
    xb_step(1)
    xb2_step(1)
    xb3_step(1)
    for d in range(2):
        for n in range(4):
            rc(grp(cb_groups[n], oc, d), grp(cb_groups[n], oc, d), cbs.at[d, n], cbr.at[d, n], dev_core).wait_recv()

    def down(n, carry):
        cc = lax.div(n, 16)
        i = lax.rem(n, 16)
        lhs, rhs = [], []
        for j in range(4):
            e = list_s[0, n * 4 + j] - cc * 64
            ey = lax.div(e, 16)
            ex = lax.rem(lax.div(e, 4), 4)
            ec = lax.rem(e, 4)
            lhs.append(plo[ey, ex, ec].reshape(128, 128))
            m = tr[cc, ey, ex, ec]
            rhs.append(jnp.concatenate([m[0], m[1]], axis=1))
        r = combine(
            jnp.dot(
                jnp.concatenate(lhs, axis=1), jnp.concatenate(rhs, axis=0), preferred_element_type=F32
            )
        )
        t = jnp.concatenate([r[:, 0].reshape(64, 128), r[:, 1].reshape(64, 128)], axis=0)
        out[cc, i] = t.T.astype(BF)
        return carry

    lax.fori_loop(0, 32, down, 0, unroll=2)
    for cp in pend:
        cp.wait_send()


def body(child_coef, transfer, child_dir, couple_src, couple_kind, couple_count, couple_table):
    dirs = child_dir.reshape(1, 128)
    active = jnp.arange(7, dtype=jnp.int32) < couple_count[..., None]
    idx = jnp.where(active, couple_kind * 64 + couple_src, ZERO_SLOT)
    idx = jnp.pad(idx, ((0, 0), (0, 0), (0, 1))).reshape(8, 16)
    idx = jnp.pad(idx, ((0, 0), (0, 112)))
    tr = transfer.reshape(2, 4, 4, 4, 2, 128, 128)
    vm = pl.BlockSpec(memory_space=pltpu.VMEM)
    dma = pltpu.SemaphoreType.DMA

    def blk(*lead):
        return pltpu.VMEM(lead + (8, 16, 128), BF)

    return pl.pallas_call(
        kernel,
        out_shape=jax.ShapeDtypeStruct((2, 16, 128, 128), BF),
        in_specs=[
            pl.BlockSpec(memory_space=pltpu.SMEM), vm, vm, vm, vm, pl.BlockSpec(memory_space=pl.ANY),
        ],
        out_specs=vm,
        scratch_shapes=[
            pltpu.VMEM((2, 4, 4, 4, 2, 128, 128), BF),
            pltpu.VMEM((2, 16, 128, 128), BF),
            blk(2, 4, 2, 4),
            blk(2, 4, 4),
            blk(2, 2, 4),
            blk(2, 2, 4),
            blk(2, 4),
            blk(2, 4),
            blk(2, 4),
            blk(2, 8),
            pltpu.VMEM((2, 8, 8, 16, 128), BF),
            pltpu.VMEM((ZERO_SLOT + 1, 16, 128), F32),
            pltpu.VMEM((2, 8, 8, 16, 128), BF),
            blk(2, 8),
            blk(2, 4),
            blk(4, 4, 4),
            pltpu.VMEM((8, 8, 128), jnp.int32),
            pltpu.SMEM((8, 8, 128), jnp.int32),
            pltpu.VMEM((8, 128), jnp.int32),
            pltpu.SMEM((8, 128), jnp.int32),
            dma((4,)), dma((2,)),
            dma((2, 4)), dma((2, 4)),
            dma((2, 2)), dma((2, 2)),
            dma((2,)), dma((2,)),
            dma((2, 2, 4)), dma((2, 2, 4)),
            dma((2, 8)), dma((2, 8)),
            dma((8,)), dma((8,)),
            dma((2, 8)), dma((2, 8)),
            dma((2, 2, 4)), dma((2, 2, 4)),
            dma((2,)), dma((2,)),
            dma((2, 2)), dma((2, 2)),
            dma((2, 4)), dma((2, 4)),
        ],
        compiler_params=pltpu.CompilerParams(
            collective_id=0, has_side_effects=True, vmem_limit_bytes=56 * 1024 * 1024
        ),
        name="h2_pass",
    )(dirs, dirs, idx, child_coef, couple_table, tr)


def solution(mesh):
    return jax.shard_map(
        body,
        mesh=mesh,
        in_specs=(
            P(("gx", "gy"), None, None, None),
            P(("gx", "gy"), None, None, None, None),
            P(("gx", "gy"), None),
            P("gx", "gy", None),
            P("gx", "gy", None),
            P("gx", "gy"),
            P("gy", None, None, None, None),
        ),
        out_specs=P(("gx", "gy"), None, None, None),
        check_vma=False,
    )
```

time: 242 us -> 89.2 us (0.37)
  Pallas kernels: 0 us -> 83.8 us
  waiting for transfers between devices: 58.5 us -> 0 us
  local copies, waits for them, and re-layouts: 54.1 us -> 4.44 us
  matrix products: 37.7 us -> 0 us
  blocking collectives: 37 us -> 0 us
  other arithmetic: 33 us -> 0.72 us
  between operations: 13.5 us -> 0.01 us
  starting transfers between devices: 7.7 us -> 0 us
    pallas_call x0 -> x1, Pallas kernels: none -> 83.8 us  [body(): pl.pallas_call(kernel, out_shape=jax.ShapeDtypeStruct((2, 16, 128, 128),...]
    dot_general x7 -> x0, matrix products: 37.7 us -> none  [the longest x3 17.7 us: complex_apply(): jnp.einsum(pattern, real_part, vectors, preferred_element_type=jnp.float32)]
    all_to_all x1 -> x0, blocking collectives: 37 us -> none  [body(): lax.all_to_all(summed, 'gy', split_axis=1, concat_axis=0, tiled=True)]
    all_gather x1 -> x0, waiting for transfers between devices: 36 us -> none  [body(): everything = lax.all_gather(parent, 'gx', axis=0, tiled=True)]
    gather x6 -> x0, local copies, waits for them, and re-layouts: 33.4 us -> none  [the longest x2 17.2 us: body(): matrices = couple_table[dir_local, couple_kind]]
    all_to_all x1 -> x0, waiting for transfers between devices: 22.5 us -> none  [body(): lax.all_to_all(copies, 'gy', split_axis=0, concat_axis=1, tiled=True)[0]]
    sub x3 -> x0, other arithmetic: 20.1 us -> none  [complex_apply(): real_term[..., :halfway] - imag_term[..., halfway:]]
    reduce_sum x3 -> x0, other arithmetic: 9.09 us -> none  [the longest x1 4.95 us: body(): summed = jnp.sum(upward, axis=0, keepdims=True).astype(jnp.bfloat16)]
  transfers between devices with their start and end apart: 2 -> 0, of which waited for: 2 -> 0; matrix products, arithmetic and copies ran while one was open for 10% -> 0% of each run, Pallas kernels for 0% -> 0%
where the time goes in v1:
time: 89.2 us; the launch traced here: 89 us
  Pallas kernels  83.8 us (94%)
  local copies, waits for them, and re-layouts  4.44 us (5%)
    pallas_call x1, Pallas kernels, body(): pl.pallas_call(kernel, out_shape=jax.ShapeDtypeStruct((2, 16, 128, 128),...  83.8 us
    unnamed x2, local copies, waits for them, and re-layouts  2.4 us

profile of v1, /device:TPU:1, one launch (start us, length us, event | category | flops | bytes accessed | tf_op | source)
XLA Modules:
  0.0 89.0 jit_solution(15824767112872561992)
XLA Ops:
  0.0 1.3 %reshape.10.dir_s.dir_v = s32[1,128]{1,0:T(1,128)} reshape(s32[2,64]{1,0:T(2,128)} %param.9) | data formatting | bytes 1024 | tf_op jit(solution)/shard_map/reshape | solution.py:337
  1.3 0.7 compare_select_fusion
  2.1 0.1 copy.9
  2.2 0.1 reshape.11
  2.3 0.6 pad.9.idx_v
  2.9 83.8 %h2_pass.1 = bf16[2,16,128,128]{3,2,1,0:T(8,128)(2,1)} custom-call(s32[1,128]{1,0:T(1,128)} %reshape.10.dir_s.dir_v, s32[1,128]{1,0:T(1,128)} %reshape.10.dir_s.dir_v, s32[8,128]{1,0:T(8,128)} %pad.9.idx_v, bf16[2,16,128,128]{3,2,1,0:T(8,128)(2,1)} %coef.1, bf16[2,8,2,128,128]{4,3,2,1,0:T(8,128)(2,1)} %table.1, bf16[2,4,4,4,2,128,128]{6,5,4,3,2,1,0:T(8,128)(2,1)} %bitcast.1), custom_call_target="tpu_custom_call" | custom-call | tf_op jit(solution)/shard_map/h2_pass/pallas_call | solution.py:349
  86.7 2.3 %copy.11 = bf16[2,16,128,128]{3,2,1,0:T(8,128)(2,1)} copy(bf16[2,16,128,128]{3,2,1,0:T(8,128)(2,1)} %h2_pass.1) | data formatting | bytes 2097152
  (1 shorter events, 0.0 us)

commit v2 on v1

--- a/solution.py
+++ b/solution.py
@@ -23,10 +23,10 @@
 
 
 def kernel(
-    dir_s, dir_v, idx_v, coef, table, tr_hbm,
+    dir_s, dir_v, src_v, kind_v, count_v, coef_hbm, table_hbm, tr_hbm,
     out,
-    tr, vc, send_own, recv_c, tx, recv_x, fw, ry_m, ry_o, rz, pz, zk, lo, qz, fd, plo,
-    idx_all, idx_s, list_v, list_s,
+    coef, table, tr, vc, send_own, recv_c, tx, recv_x, fw, ry_m, ry_o, rz, pz, zk, lo, qz, fd, plo,
+    idx_v, idx_all, idx_s, list_v, list_s,
     sem_ld, sem_sm,
     cs, cr, xs, xr, fs, fr, ys, yr, zs, zr, is_, ir,
     zbs, zbr, ybs, ybr, fbs, fbr, xbs, xbr, cbs, cbr,
@@ -81,11 +81,22 @@
     for dev in partners:
         pl.semaphore_signal(barrier, inc=1, device_id=dev, device_id_type=MESH)
 
+    cp_coef = pltpu.make_async_copy(coef_hbm, coef, sem_ld.at[4])
+    cp_coef.start()
     loads = []
     for k in range(4):
         cp = pltpu.make_async_copy(tr_hbm.at[:, :, pri[k]], tr.at[:, :, pri[k]], sem_ld.at[k])
         cp.start()
         loads.append(cp)
+
+    cp_table = pltpu.make_async_copy(table_hbm, table, sem_ld.at[5])
+    cp_table.start()
+
+    for m in range(7):
+        idx_v[2 * m : 2 * m + 2, 0:8] = jnp.where(
+            count_v[...] > m, kind_v[m] * 64 + src_v[m], ZERO_SLOT
+        )
+    cp_coef.wait()
 
     def prep(n, carry):
         cc = lax.div(n, 16)
@@ -95,7 +106,7 @@
         vc[cc, i] = v.reshape(128, 128).astype(BF)
         return carry
 
-    lax.fori_loop(0, 32, prep, 0, unroll=2)
+    lax.fori_loop(0, 32, prep, 0, unroll=4)
 
     pl.semaphore_wait(barrier, len(partners))
 
@@ -110,7 +121,7 @@
             cc = lax.rem(oc + first, 2)
             cd = cc * 2 + d
             e = yy * 16 + pri[k] * 4 + cd
-            lhs = jnp.concatenate([vc[0, dir_s[0, e]], vc[1, dir_s[0, 64 + e]]], axis=1)
+            lhs = jnp.concatenate([vc[0, dir_s[0, e]], vc[1, dir_s[1, e]]], axis=1)
             rhs = jnp.concatenate(
                 [tr[0, yy, pri[k], cd].reshape(256, 128), tr[1, yy, pri[k], cd].reshape(256, 128)], axis=1
             )
@@ -118,7 +129,7 @@
             send_own[d, k, first, yy] = r.reshape(8, 16, 128).astype(BF)
             return carry
 
-        lax.fori_loop(0, 8, one, 0, unroll=2)
+        lax.fori_loop(0, 8, one, 0, unroll=8)
 
 
     def core_send(d, k):
@@ -191,14 +202,14 @@
             if pk < 2:
                 t_step(pd, pk)
 
-    row = jnp.broadcast_to(dir_v[...], (128, 128))
     lane = lax.broadcasted_iota(jnp.int32, (128, 128), 1)
     sub = lax.broadcasted_iota(jnp.int32, (128, 128), 0)
-    row = row + jnp.where(lane >= 64, 16, 0)
-    same = jnp.where((row == row.T) & (sub < lane), 1, 0)
-    key = row * 4 + jnp.broadcast_to(jnp.sum(same, axis=0, keepdims=True), (128, 128))
-    lst = jnp.sum(jnp.where(key.T == lane, sub, 0), axis=0, keepdims=True)
-    list_v[...] = jnp.broadcast_to(lst, (8, 128))
+    for cc in range(2):
+        list_v[cc : cc + 1, 0:64] = dir_v[cc : cc + 1, :]
+        row = jnp.where(lane < 64, jnp.broadcast_to(list_v[cc : cc + 1, :], (128, 128)), 64)
+        same = jnp.where((row == row.T) & (sub < lane), 1, 0)
+        key = row * 4 + jnp.broadcast_to(jnp.sum(same, axis=0, keepdims=True), (128, 128))
+        list_v[cc : cc + 1, :] = jnp.sum(jnp.where(key.T == lane, sub, 0), axis=0, keepdims=True)
     zk[ZERO_SLOT] = jnp.zeros((16, 128), F32)
 
     f_step(0)
@@ -218,34 +229,33 @@
     cp_idx.start()
     z_send(1)
     cp_idx.wait()
+    cp_table.wait()
 
     def couple(d):
         for dz in ZS:
             zz = zo(dz)
             rc(rz.at[d, :, zz], pz.at[d, zz], zs.at[d, zz], zr.at[d, zz], dev_z(zz)).wait_recv()
 
-        def dense(n, carry):
-            k = lax.div(n, 4)
-            q = lax.rem(n, 4)
-            lhs = pz[d, pl.ds(q * 2, 2)].reshape(256, 128)
-            r = combine(
-                lax.dot_general(lhs, table[d, k].reshape(256, 128), NT, preferred_element_type=F32)
-            )
-            zk[pl.ds(n * 16, 16)] = r.reshape(16, 16, 128)
+        def dense(k, carry):
+            rhs = table[d, k].reshape(256, 128)
+            for q in range(4):
+                lhs = pz[d, q * 2 : q * 2 + 2].reshape(256, 128)
+                r = combine(lax.dot_general(lhs, rhs, NT, preferred_element_type=F32))
+                zk[pl.ds(k * 64 + q * 16, 16)] = r.reshape(16, 16, 128)
             return carry
 
-        lax.fori_loop(0, 32, dense, 0)
+        lax.fori_loop(0, 8, dense, 0, unroll=2)
         for dz in ZS + (0,):
             zz = zo(dz)
 
             def row_sum(p, carry):
-                acc = zk[idx_s[zz, p, d * 8]]
+                acc = zk[idx_s[zz, d, p]]
                 for m in range(1, 7):
-                    acc = acc + zk[idx_s[zz, p, d * 8 + m]]
+                    acc = acc + zk[idx_s[zz, 2 * m + d, p]]
                 lo[d, zz, p] = acc.astype(BF)
                 return carry
 
-            lax.fori_loop(0, 8, row_sum, 0, unroll=2)
+            lax.fori_loop(0, 8, row_sum, 0, unroll=4)
             if dz:
                 go(rc(lo.at[d, zz], qz.at[d, :, z], zbs.at[d, zz], zbr.at[d, z], dev_z(zz)))
         qz[d, :, z] = lo[d, z]
@@ -312,7 +322,7 @@
         i = lax.rem(n, 16)
         lhs, rhs = [], []
         for j in range(4):
-            e = list_s[0, n * 4 + j] - cc * 64
+            e = list_s[cc, i * 4 + j]
             ey = lax.div(e, 16)
             ex = lax.rem(lax.div(e, 4), 4)
             ec = lax.rem(e, 4)
@@ -328,19 +338,17 @@
         out[cc, i] = t.T.astype(BF)
         return carry
 
-    lax.fori_loop(0, 32, down, 0, unroll=2)
+    lax.fori_loop(0, 32, down, 0, unroll=4)
     for cp in pend:
         cp.wait_send()
 
 
 def body(child_coef, transfer, child_dir, couple_src, couple_kind, couple_count, couple_table):
-    dirs = child_dir.reshape(1, 128)
-    active = jnp.arange(7, dtype=jnp.int32) < couple_count[..., None]
-    idx = jnp.where(active, couple_kind * 64 + couple_src, ZERO_SLOT)
-    idx = jnp.pad(idx, ((0, 0), (0, 0), (0, 1))).reshape(8, 16)
-    idx = jnp.pad(idx, ((0, 0), (0, 112)))
+    flip = (2, 1, 0)
+    src, kind = couple_src.transpose(flip), couple_kind.transpose(flip)
     tr = transfer.reshape(2, 4, 4, 4, 2, 128, 128)
     vm = pl.BlockSpec(memory_space=pltpu.VMEM)
+    hbm = pl.BlockSpec(memory_space=pl.ANY)
     dma = pltpu.SemaphoreType.DMA
 
     def blk(*lead):
@@ -348,12 +356,12 @@
 
     return pl.pallas_call(
         kernel,
-        out_shape=jax.ShapeDtypeStruct((2, 16, 128, 128), BF),
-        in_specs=[
-            pl.BlockSpec(memory_space=pltpu.SMEM), vm, vm, vm, vm, pl.BlockSpec(memory_space=pl.ANY),
-        ],
+        out_shape=pltpu.VMEM((2, 16, 128, 128), BF),
+        in_specs=[pl.BlockSpec(memory_space=pltpu.SMEM), vm, vm, vm, vm, hbm, hbm, hbm],
         out_specs=vm,
         scratch_shapes=[
+            pltpu.VMEM((2, 16, 128, 128), BF),
+            pltpu.VMEM((2, 8, 2, 128, 128), BF),
             pltpu.VMEM((2, 4, 4, 4, 2, 128, 128), BF),
             pltpu.VMEM((2, 16, 128, 128), BF),
             blk(2, 4, 2, 4),
@@ -370,11 +378,12 @@
             blk(2, 8),
             blk(2, 4),
             blk(4, 4, 4),
-            pltpu.VMEM((8, 8, 128), jnp.int32),
-            pltpu.SMEM((8, 8, 128), jnp.int32),
+            pltpu.VMEM((16, 128), jnp.int32),
+            pltpu.VMEM((8, 16, 128), jnp.int32),
+            pltpu.SMEM((8, 16, 128), jnp.int32),
             pltpu.VMEM((8, 128), jnp.int32),
             pltpu.SMEM((8, 128), jnp.int32),
-            dma((4,)), dma((2,)),
+            dma((6,)), dma((2,)),
             dma((2, 4)), dma((2, 4)),
             dma((2, 2)), dma((2, 2)),
             dma((2,)), dma((2,)),
@@ -391,7 +400,7 @@
             collective_id=0, has_side_effects=True, vmem_limit_bytes=56 * 1024 * 1024
         ),
         name="h2_pass",
-    )(dirs, dirs, idx, child_coef, couple_table, tr)
+    )(child_dir, child_dir, src, kind, couple_count.T, child_coef, couple_table, tr)
 
 
 def solution(mesh):

time: 89.2 us -> 76 us (0.85)
  Pallas kernels: 83.8 us -> 74.9 us
  local copies, waits for them, and re-layouts: 4.44 us -> 0.97 us
    pallas_call x1, Pallas kernels: 83.8 us -> 74.9 us  [body(): pl.pallas_call(kernel, out_shape=pltpu.VMEM((2, 16, 128, 128), BF), in_sp...]
    unnamed x2 -> x1, local copies, waits for them, and re-layouts: 2.4 us -> 0.97 us
    reshape x2 -> x0, local copies, waits for them, and re-layouts: 1.43 us -> none  [the longest x1 1.35 us: body(): dirs = child_dir.reshape(1, 128)]
where the time goes in v2:
time: 76 us; the launch traced here: 75.9 us
  Pallas kernels  74.9 us (99%)
  local copies, waits for them, and re-layouts  0.97 us (1%)
    pallas_call x1, Pallas kernels, body(): pl.pallas_call(kernel, out_shape=pltpu.VMEM((2, 16, 128, 128), BF), in_sp...  74.9 us

profile of v2, /device:TPU:1, one launch (start us, length us, event | category | flops | bytes accessed | tf_op | source)
XLA Modules:
  0.0 75.9 jit_solution(4013791727888533978)
XLA Ops:
  0.0 74.9 %h2_pass.1 = bf16[2,16,128,128]{3,2,1,0:T(8,128)(2,1)S(1)} custom-call(s32[2,64]{1,0:T(2,128)} %dir_v.1, s32[2,64]{1,0:T(2,128)} %dir_v.1, s32[7,2,8]{2,1,0:T(2,128)} %bitcast.5, s32[7,2,8]{2,1,0:T(2,128)} %bitcast.6, s32[2,8]{1,0:T(2,128)} %bitcast.7, bf16[2,16,128,128]{3,2,1,0:T(8,128)(2,1)} %coef_hbm.1, bf16[2,8,2,128,128]{4,3,2,1,0:T(8,128)(2,1)} %table_hbm.1, ...), custom_call_target="tpu_custom_call" | custom-call | tf_op jit(solution)/shard_map/h2_pass/pallas_call | solution.py:357
  74.9 1.0 %copy.9 = bf16[2,16,128,128]{3,2,1,0:T(8,128)(2,1)} copy(bf16[2,16,128,128]{3,2,1,0:T(8,128)(2,1)S(1)} %h2_pass.1) | data formatting | bytes 2097152

commit v3 on v2

v3 whole, which is shorter than its diff:
```python
import jax
import jax.numpy as jnp
from jax import lax
from jax.experimental import pallas as pl
from jax.experimental.pallas import tpu as pltpu
from jax.sharding import PartitionSpec as P

MESH = pl.DeviceIdType.MESH
NT = (((1,), (1,)), ((), ()))
BF = jnp.bfloat16
F32 = jnp.float32
ZERO_SLOT = 512


def combine(z):
    z = z.reshape(z.shape[0] // 16, 2, 8, 256)
    re, im = z[:, 0], z[:, 1]
    out_re = re[:, :, :128] - im[:, :, 128:]
    out_im = im[:, :, :128] + re[:, :, 128:]
    return jnp.concatenate([out_re[:, None], out_im[:, None]], axis=1)


def kernel(
    dir_s, dir_v, src_v, kind_v, count_v, coef_hbm, table_hbm, tr_hbm,
    out,
    coef, table, tr, vc, send_own, recv_c, tx, recv_x, fw, ry_m, ry_o, rz, pz, zk, lo, qz, fd, plo,
    idx_v, idx_all, idx_s, list_v, list_s,
    sem_ld, sem_sm,
    cs, cr, xs, xr, fs, fr, ys, yr, zs, zr, is_, ir,
    zbs, zbr, ybs, ybr, fbs, fbr, xbs, xbr, cbs, cbr,
):
    z = lax.axis_index("gx")
    g = lax.axis_index("gy")
    c = lax.rem(g, 2)
    x = lax.rem(lax.div(g, 2), 4)
    y = lax.div(g, 8)
    xp = x + 1 - 2 * lax.rem(x, 2)
    xn = 3 - x
    xf = 3 - xp
    xh = lax.div(x, 2)
    oc = 1 - c

    def gid(yy, xx, cc):
        return (yy * 4 + xx) * 2 + cc

    dev_core = (z, gid(y, x, oc))
    dev_xp = (z, gid(y, xp, c))
    dev_xn = (z, gid(y, xn, c))

    def yo(dy):
        return lax.rem(y + dy, 4)

    def zo(dz):
        return lax.rem(z + dz, 8)

    def dev_y(yy):
        return (z, gid(yy, x, c))

    def dev_z(zz):
        return (zz, g)

    def rc(src, dst, ss, rs, dev):
        return pltpu.make_async_remote_copy(
            src_ref=src, dst_ref=dst, send_sem=ss, recv_sem=rs, device_id=dev, device_id_type=MESH
        )

    pend = []

    def go(cp):
        cp.start()
        pend.append(cp)

    YS = (2, 1, 3)
    ZE = (4, 2, 6)
    ZO = (3, 5, 1, 7)
    ZR = (ZE, ZO)
    ZS = ZE + ZO
    pri = (xf, xp, xn, x)

    def slot(h):
        return lax.rem(z + h, 2)

    barrier = pltpu.get_barrier_semaphore()
    partners = [dev_core, dev_xp, dev_xn] + [dev_y(yo(dy)) for dy in YS] + [dev_z(zo(dz)) for dz in ZS]
    for dev in partners:
        pl.semaphore_signal(barrier, inc=1, device_id=dev, device_id_type=MESH)

    cp_coef = pltpu.make_async_copy(coef_hbm, coef, sem_ld.at[4])
    cp_coef.start()
    loads = []
    for k in range(4):
        cp = pltpu.make_async_copy(tr_hbm.at[:, :, pri[k]], tr.at[:, :, pri[k]], sem_ld.at[k])
        cp.start()
        loads.append(cp)

    cp_table = pltpu.make_async_copy(table_hbm, table, sem_ld.at[5])
    cp_table.start()

    for m in range(7):
        idx_v[2 * m : 2 * m + 2, 0:8] = jnp.where(
            count_v[...] > m, kind_v[m] * 64 + src_v[m], ZERO_SLOT
        )
    cp_coef.wait()

    def prep(n, carry):
        cc = lax.div(n, 16)
        i = lax.rem(n, 16)
        vt = coef[cc, i].astype(F32).T.reshape(2, 8, 8, 128)
        v = jnp.concatenate([vt[0][:, None], vt[1][:, None]], axis=1)
        vc[cc, i] = v.reshape(128, 128).astype(BF)
        return carry

    lax.fori_loop(0, 32, prep, 0, unroll=4)

    def up(d, k):
        def one(n, carry):
            yy = lax.rem(n, 4)
            first = lax.div(n, 4)
            cc = lax.rem(oc + first, 2)
            cd = cc * 2 + d
            e = yy * 16 + pri[k] * 4 + cd
            lhs = jnp.concatenate([vc[0, dir_s[0, e]], vc[1, dir_s[1, e]]], axis=1)
            rhs = jnp.concatenate(
                [tr[0, yy, pri[k], cd].reshape(256, 128), tr[1, yy, pri[k], cd].reshape(256, 128)], axis=1
            )
            r = combine(lax.dot_general(lhs, rhs, NT, preferred_element_type=F32))
            r = r.reshape(8, 16, 128).astype(BF)
            for h in range(2):
                send_own[d, slot(h), k, first, yy] = r[4 * h : 4 * h + 4]
            return carry

        lax.fori_loop(0, 8, one, 0, unroll=8)

    def core_copy(d, k):
        return rc(send_own.at[d, :, k, 0], recv_c.at[d, :, k], cs.at[d, k], cr.at[d, k], dev_core)

    def x_copy(d, r, k):
        return rc(tx.at[d, r, k], recv_x.at[d, r, k], xs.at[d, r, k], xr.at[d, r, k], dev_xp)

    def fw_copy(d, r):
        return rc(fw.at[d, r], ry_o.at[d, r], fs.at[d, r], fr.at[d, r], dev_xn)

    def t_step(d, k):
        core_copy(d, k).wait_recv()
        for r in range(2):
            tx[d, r, k] = (send_own[d, r, k, 1].astype(F32) + recv_c[d, r, k].astype(F32)).astype(BF)
            go(x_copy(d, r, k))

    def add3(d, r, k):
        return (
            send_own[d, r, k + 2, 1].astype(F32)
            + recv_c[d, r, k + 2].astype(F32)
            + recv_x[d, r, k].astype(F32)
        ).astype(BF)

    def f_step(d, r):
        if r == 0:
            core_copy(d, 2).wait_recv()
        x_copy(d, r, 0).wait_recv()
        fw[d, r] = add3(d, r, 0)
        go(fw_copy(d, r))

    def y_copy(d, r, kind, src, yy, arrive):
        p = (yy if arrive else y) * 2 + (xh if kind == 0 else 1 - xh)
        return rc(
            src.at[d, r, yy], rz.at[d, r, p],
            ys.at[d, r, kind, yy], yr.at[d, r, kind, yy if arrive else y], dev_y(yy),
        )

    def g_step(d, r):
        if r == 0:
            core_copy(d, 3).wait_recv()
        x_copy(d, r, 1).wait_recv()
        ry_m[d, r] = add3(d, r, 1)
        for dy in YS:
            go(y_copy(d, r, 0, ry_m, yo(dy), False))
        rz[d, r, y * 2 + xh] = ry_m[d, r, y]

    def h_step(d, r):
        fw_copy(d, r).wait_recv()
        for dy in YS:
            go(y_copy(d, r, 1, ry_o, yo(dy), False))
        rz[d, r, y * 2 + 1 - xh] = ry_o[d, r, y]

    def z_copy(d, dz, arrive):
        zz = zo(dz)
        zf = zz if arrive else z
        return rc(
            rz.at[d, dz % 2, :, lax.div(zz, 2)], pz.at[d, zf], zs.at[d, zz], zr.at[d, zf], dev_z(zz)
        )

    def z_send(d, r):
        for kind in range(2):
            for dy in YS:
                y_copy(d, r, kind, ry_m, yo(dy), True).wait_recv()
        for dz in ZR[r]:
            go(z_copy(d, dz, False))
        if r == 0:
            pz[d, z] = rz[d, 0, :, lax.div(z, 2)]

    def idx_copy(dz, arrive):
        zz = zo(dz)
        zf = zz if arrive else z
        return rc(idx_v, idx_all.at[zf], is_.at[zz], ir.at[zf], dev_z(zz))

    loads[0].wait()
    up(0, 0)
    pl.semaphore_wait(barrier, len(partners))
    go(core_copy(0, 0))
    loads[1].wait()
    up(0, 1)
    go(core_copy(0, 1))
    t_step(0, 0)
    loads[2].wait()
    up(0, 2)
    go(core_copy(0, 2))
    t_step(0, 1)
    for dz in ZS:
        go(idx_copy(dz, False))
    idx_all[z] = idx_v[...]
    loads[3].wait()
    up(0, 3)
    go(core_copy(0, 3))
    up(1, 0)
    go(core_copy(1, 0))
    f_step(0, 0)
    up(1, 1)
    go(core_copy(1, 1))
    f_step(0, 1)
    t_step(1, 0)
    up(1, 2)
    go(core_copy(1, 2))
    t_step(1, 1)
    g_step(0, 0)
    h_step(0, 0)
    up(1, 3)
    go(core_copy(1, 3))
    g_step(0, 1)
    h_step(0, 1)
    f_step(1, 0)

    lane = lax.broadcasted_iota(jnp.int32, (128, 128), 1)
    sub = lax.broadcasted_iota(jnp.int32, (128, 128), 0)
    for cc in range(2):
        list_v[cc : cc + 1, 0:64] = dir_v[cc : cc + 1, :]
        row = jnp.where(lane < 64, jnp.broadcast_to(list_v[cc : cc + 1, :], (128, 128)), 64)
        same = jnp.where((row == row.T) & (sub < lane), 1, 0)
        key = row * 4 + jnp.broadcast_to(jnp.sum(same, axis=0, keepdims=True), (128, 128))
        list_v[cc : cc + 1, :] = jnp.sum(jnp.where(key.T == lane, sub, 0), axis=0, keepdims=True)
    zk[ZERO_SLOT] = jnp.zeros((16, 128), F32)

    z_send(0, 0)
    f_step(1, 1)
    cp_list = pltpu.make_async_copy(list_v, list_s, sem_sm.at[0])
    cp_list.start()
    z_send(0, 1)
    g_step(1, 0)
    h_step(1, 0)
    g_step(1, 1)
    h_step(1, 1)
    cp_list.wait()
    for dz in ZS:
        idx_copy(dz, True).wait_recv()
    cp_idx = pltpu.make_async_copy(idx_all, idx_s, sem_sm.at[1])
    cp_idx.start()
    z_send(1, 0)
    cp_idx.wait()
    cp_table.wait()
    z_send(1, 1)

    def zb_copy(d, dz, arrive):
        zz = zo(dz)
        zf = zz if arrive else z
        return rc(
            lo.at[d, zz], qz.at[d, dz % 2, :, lax.div(zf, 2)], zbs.at[d, zz], zbr.at[d, zf], dev_z(zz)
        )

    def couple(d):
        for dz in ZS:
            z_copy(d, dz, True).wait_recv()

        def dense(k, carry):
            rhs = table[d, k].reshape(256, 128)
            for q in range(4):
                lhs = pz[d, q * 2 : q * 2 + 2].reshape(256, 128)
                r = combine(lax.dot_general(lhs, rhs, NT, preferred_element_type=F32))
                zk[pl.ds(k * 64 + q * 16, 16)] = r.reshape(16, 16, 128)
            return carry

        lax.fori_loop(0, 8, dense, 0, unroll=2)
        for dz in ZE + (0,) + ZO:
            zz = zo(dz)

            def row_sum(p, carry):
                acc = zk[idx_s[zz, d, p]]
                for m in range(1, 7):
                    acc = acc + zk[idx_s[zz, 2 * m + d, p]]
                lo[d, zz, p] = acc.astype(BF)
                return carry

            lax.fori_loop(0, 8, row_sum, 0, unroll=4)
            if dz:
                go(zb_copy(d, dz, False))
        qz[d, 0, :, lax.div(z, 2)] = lo[d, z]

    def yb_copy(d, r, kind, yy, arrive):
        yf = yy if arrive else y
        p = yy * 2 + (xh if kind == 0 else 1 - xh)
        dst = plo.at[r, yf, x, c * 2 + d] if kind == 0 else fd.at[d, r, yf]
        return rc(qz.at[d, r, p], dst, ybs.at[d, r, kind, yy], ybr.at[d, r, kind, yf], dev_y(yy))

    def yb_step(d, r):
        for dz in ZR[r]:
            zb_copy(d, dz, True).wait_recv()
        for kind in (1, 0):
            for dy in YS:
                go(yb_copy(d, r, kind, yo(dy), False))
        fd[d, r, y] = qz[d, r, y * 2 + 1 - xh]
        plo[r, y, x, c * 2 + d] = qz[d, r, y * 2 + xh]

    def grp(r, xx, cc, d):
        return plo.at[r, :, xx, cc * 2 + d]

    cb_groups = (x, xn, xp, xf)

    def cb_copy(d, r, n, cc):
        ref = grp(r, cb_groups[n], cc, d)
        return rc(ref, ref, cbs.at[d, r, n], cbr.at[d, r, n], dev_core)

    def fb_copy(d, r, xx):
        return rc(fd.at[d, r], grp(r, xx, c, d), fbs.at[d, r], fbr.at[d, r], dev_xn)

    def xb_copy(d, r, n, src, dst):
        return rc(grp(r, src, c, d), grp(r, dst, c, d), xbs.at[d, r, n], xbr.at[d, r, n], dev_xp)

    def xb_step(d, r):
        for dy in YS:
            yb_copy(d, r, 1, yo(dy), True).wait_recv()
        go(fb_copy(d, r, x))
        for dy in YS:
            yb_copy(d, r, 0, yo(dy), True).wait_recv()
        go(xb_copy(d, r, 0, x, x))
        go(cb_copy(d, r, 0, c))

    def xb2_step(d, r):
        fb_copy(d, r, xn).wait_recv()
        go(xb_copy(d, r, 1, xn, xn))
        go(cb_copy(d, r, 1, c))

    def xb3_step(d, r):
        xb_copy(d, r, 0, x, xp).wait_recv()
        go(cb_copy(d, r, 2, c))
        xb_copy(d, r, 1, xn, xf).wait_recv()
        go(cb_copy(d, r, 3, c))

    couple(0)
    couple(1)
    yb_step(0, 0)
    yb_step(0, 1)
    xb_step(0, 0)
    yb_step(1, 0)
    xb_step(0, 1)
    xb2_step(0, 0)
    yb_step(1, 1)
    xb_step(1, 0)
    xb2_step(0, 1)
    xb3_step(0, 0)
    xb_step(1, 1)
    xb2_step(1, 0)
    xb3_step(0, 1)
    xb2_step(1, 1)
    xb3_step(1, 0)
    xb3_step(1, 1)
    for d in range(2):
        for r in range(2):
            for n in range(4):
                cb_copy(d, r, n, oc).wait_recv()

    def down(n, carry):
        cc = lax.div(n, 16)
        i = lax.rem(n, 16)
        lhs, rhs = [], []
        for j in range(4):
            e = list_s[cc, i * 4 + j]
            ey = lax.div(e, 16)
            ex = lax.rem(lax.div(e, 4), 4)
            ec = lax.rem(e, 4)
            halves = [plo[slot(h), ey, ex, ec].reshape(64, 128) for h in range(2)]
            lhs.append(jnp.concatenate(halves, axis=0))
            m = tr[cc, ey, ex, ec]
            rhs.append(jnp.concatenate([m[0], m[1]], axis=1))
        r = combine(
            jnp.dot(
                jnp.concatenate(lhs, axis=1), jnp.concatenate(rhs, axis=0), preferred_element_type=F32
            )
        )
        t = jnp.concatenate([r[:, 0].reshape(64, 128), r[:, 1].reshape(64, 128)], axis=0)
        out[cc, i] = t.T.astype(BF)
        return carry

    lax.fori_loop(0, 32, down, 0, unroll=4)
    for cp in pend:
        cp.wait_send()


def body(child_coef, transfer, child_dir, couple_src, couple_kind, couple_count, couple_table):
    flip = (2, 1, 0)
    src, kind = couple_src.transpose(flip), couple_kind.transpose(flip)
    tr = transfer.reshape(2, 4, 4, 4, 2, 128, 128)
    vm = pl.BlockSpec(memory_space=pltpu.VMEM)
    hbm = pl.BlockSpec(memory_space=pl.ANY)
    dma = pltpu.SemaphoreType.DMA

    def blk(*lead):
        return pltpu.VMEM(lead + (4, 16, 128), BF)

    return pl.pallas_call(
        kernel,
        out_shape=pltpu.VMEM((2, 16, 128, 128), BF),
        in_specs=[pl.BlockSpec(memory_space=pltpu.SMEM), vm, vm, vm, vm, hbm, hbm, hbm],
        out_specs=vm,
        scratch_shapes=[
            pltpu.VMEM((2, 16, 128, 128), BF),
            pltpu.VMEM((2, 8, 2, 128, 128), BF),
            pltpu.VMEM((2, 4, 4, 4, 2, 128, 128), BF),
            pltpu.VMEM((2, 16, 128, 128), BF),
            blk(2, 2, 4, 2, 4),
            blk(2, 2, 4, 4),
            blk(2, 2, 2, 4),
            blk(2, 2, 2, 4),
            blk(2, 2, 4),
            blk(2, 2, 4),
            blk(2, 2, 4),
            blk(2, 2, 8),
            pltpu.VMEM((2, 8, 8, 16, 128), BF),
            pltpu.VMEM((ZERO_SLOT + 1, 16, 128), F32),
            pltpu.VMEM((2, 8, 8, 16, 128), BF),
            blk(2, 2, 8),
            blk(2, 2, 4),
            blk(2, 4, 4, 4),
            pltpu.VMEM((16, 128), jnp.int32),
            pltpu.VMEM((8, 16, 128), jnp.int32),
            pltpu.SMEM((8, 16, 128), jnp.int32),
            pltpu.VMEM((8, 128), jnp.int32),
            pltpu.SMEM((8, 128), jnp.int32),
            dma((6,)), dma((2,)),
            dma((2, 4)), dma((2, 4)),
            dma((2, 2, 2)), dma((2, 2, 2)),
            dma((2, 2)), dma((2, 2)),
            dma((2, 2, 2, 4)), dma((2, 2, 2, 4)),
            dma((2, 8)), dma((2, 8)),
            dma((8,)), dma((8,)),
            dma((2, 8)), dma((2, 8)),
            dma((2, 2, 2, 4)), dma((2, 2, 2, 4)),
            dma((2, 2)), dma((2, 2)),
            dma((2, 2, 2)), dma((2, 2, 2)),
            dma((2, 2, 4)), dma((2, 2, 4)),
        ],
        compiler_params=pltpu.CompilerParams(
            collective_id=0, has_side_effects=True, vmem_limit_bytes=56 * 1024 * 1024
        ),
        name="h2_pass",
    )(child_dir, child_dir, src, kind, couple_count.T, child_coef, couple_table, tr)


def solution(mesh):
    return jax.shard_map(
        body,
        mesh=mesh,
        in_specs=(
            P(("gx", "gy"), None, None, None),
            P(("gx", "gy"), None, None, None, None),
            P(("gx", "gy"), None),
            P("gx", "gy", None),
            P("gx", "gy", None),
            P("gx", "gy"),
            P("gy", None, None, None, None),
        ),
        out_specs=P(("gx", "gy"), None, None, None),
        check_vma=False,
    )
```

time: 76 us -> 68.6 us (0.903)
  Pallas kernels: 74.9 us -> 67.5 us
    pallas_call x1, Pallas kernels: 74.9 us -> 67.5 us  [body(): pl.pallas_call(kernel, out_shape=pltpu.VMEM((2, 16, 128, 128), BF), in_sp...]
where the time goes in v3:
time: 68.6 us; the launch traced here: 68.5 us
  Pallas kernels  67.5 us (98%)
  local copies, waits for them, and re-layouts  0.97 us (1%)
    pallas_call x1, Pallas kernels, body(): pl.pallas_call(kernel, out_shape=pltpu.VMEM((2, 16, 128, 128), BF), in_sp...  67.5 us

profile of v3, /device:TPU:1, one launch (start us, length us, event | category | flops | bytes accessed | tf_op | source)
XLA Modules:
  0.0 68.5 jit_solution(5124521893389241178)
XLA Ops:
  0.0 67.5 %h2_pass.1 = bf16[2,16,128,128]{3,2,1,0:T(8,128)(2,1)S(1)} custom-call(s32[2,64]{1,0:T(2,128)} %dir_v.1, s32[2,64]{1,0:T(2,128)} %dir_v.1, s32[7,2,8]{2,1,0:T(2,128)} %bitcast.5, s32[7,2,8]{2,1,0:T(2,128)} %bitcast.6, s32[2,8]{1,0:T(2,128)} %bitcast.7, bf16[2,16,128,128]{3,2,1,0:T(8,128)(2,1)} %coef_hbm.1, bf16[2,8,2,128,128]{4,3,2,1,0:T(8,128)(2,1)} %table_hbm.1, ...), custom_call_target="tpu_custom_call" | custom-call | tf_op jit(solution)/shard_map/h2_pass/pallas_call | solution.py:417
  67.5 1.0 %copy.9 = bf16[2,16,128,128]{3,2,1,0:T(8,128)(2,1)} copy(bf16[2,16,128,128]{3,2,1,0:T(8,128)(2,1)S(1)} %h2_pass.1) | data formatting | bytes 2097152

commit v4 on v3

--- a/solution.py
+++ b/solution.py
@@ -23,11 +23,11 @@
 def kernel(
     dir_s, dir_v, src_v, kind_v, count_v, coef_hbm, table_hbm, tr_hbm,
     out,
-    coef, table, tr, vc, send_own, recv_c, tx, recv_x, fw, ry_m, ry_o, rz, pz, zk, lo, qz, fd, plo,
+    coef, table, tr, vc, send_own, recv_c, tx, recv_x, fw, ry_m, rz, pz, zk, lo, qz, plo,
     idx_v, idx_all, idx_s, list_v, list_s,
     sem_ld, sem_sm,
-    cs, cr, xs, xr, fs, fr, ys, yr, zs, zr, is_, ir,
-    zbs, zbr, ybs, ybr, fbs, fbr, xbs, xbr, cbs, cbr,
+    cs, cr, xs, xr, ys, yr, zs, zr, is_, ir,
+    zbs, zbr, ybs, ybr, cbs, cbr,
 ):
     z = lax.axis_index("gx")
     g = lax.axis_index("gy")
@@ -45,7 +45,6 @@
 
     dev_core = (z, gid(y, x, oc))
     dev_xp = (z, gid(y, xp, c))
-    dev_xn = (z, gid(y, xn, c))
 
     def yo(dy):
         return lax.rem(y + dy, 4)
@@ -53,8 +52,10 @@
     def zo(dz):
         return lax.rem(z + dz, 8)
 
-    def dev_y(yy):
-        return (z, gid(yy, x, c))
+    rel = (x, xp, xn, xf)
+
+    def dev_n(n, dy):
+        return (z, gid(yo(dy), rel[n], c))
 
     def dev_z(zz):
         return (zz, g)
@@ -81,7 +82,8 @@
         return lax.rem(z + h, 2)
 
     barrier = pltpu.get_barrier_semaphore()
-    partners = [dev_core, dev_xp, dev_xn] + [dev_y(yo(dy)) for dy in YS] + [dev_z(zo(dz)) for dz in ZS]
+    partners = [dev_core] + [dev_z(zo(dz)) for dz in ZS]
+    partners += [dev_n(n, dy) for n in range(4) for dy in range(4) if n or dy]
     for dev in partners:
         pl.semaphore_signal(barrier, inc=1, device_id=dev, device_id_type=MESH)
 
@@ -137,9 +139,6 @@
     def x_copy(d, r, k):
         return rc(tx.at[d, r, k], recv_x.at[d, r, k], xs.at[d, r, k], xr.at[d, r, k], dev_xp)
 
-    def fw_copy(d, r):
-        return rc(fw.at[d, r], ry_o.at[d, r], fs.at[d, r], fr.at[d, r], dev_xn)
-
     def t_step(d, k):
         core_copy(d, k).wait_recv()
         for r in range(2):
@@ -153,19 +152,22 @@
             + recv_x[d, r, k].astype(F32)
         ).astype(BF)
 
+    def y_copy(d, r, n, dy, arrive):
+        yy = yo(dy)
+        yf = yy if arrive else y
+        src = fw if n else ry_m
+        p = yf * 2 + (1 - xh if n and arrive else xh)
+        return rc(
+            src.at[d, r, yy], rz.at[d, r, p], ys.at[d, r, n // 2, yy], yr.at[d, r, n // 2, yf], dev_n(n, dy)
+        )
+
     def f_step(d, r):
         if r == 0:
             core_copy(d, 2).wait_recv()
         x_copy(d, r, 0).wait_recv()
         fw[d, r] = add3(d, r, 0)
-        go(fw_copy(d, r))
-
-    def y_copy(d, r, kind, src, yy, arrive):
-        p = (yy if arrive else y) * 2 + (xh if kind == 0 else 1 - xh)
-        return rc(
-            src.at[d, r, yy], rz.at[d, r, p],
-            ys.at[d, r, kind, yy], yr.at[d, r, kind, yy if arrive else y], dev_y(yy),
-        )
+        for dy in YS + (0,):
+            go(y_copy(d, r, 2, dy, False))
 
     def g_step(d, r):
         if r == 0:
@@ -173,14 +175,8 @@
         x_copy(d, r, 1).wait_recv()
         ry_m[d, r] = add3(d, r, 1)
         for dy in YS:
-            go(y_copy(d, r, 0, ry_m, yo(dy), False))
+            go(y_copy(d, r, 0, dy, False))
         rz[d, r, y * 2 + xh] = ry_m[d, r, y]
-
-    def h_step(d, r):
-        fw_copy(d, r).wait_recv()
-        for dy in YS:
-            go(y_copy(d, r, 1, ry_o, yo(dy), False))
-        rz[d, r, y * 2 + 1 - xh] = ry_o[d, r, y]
 
     def z_copy(d, dz, arrive):
         zz = zo(dz)
@@ -190,9 +186,10 @@
         )
 
     def z_send(d, r):
-        for kind in range(2):
-            for dy in YS:
-                y_copy(d, r, kind, ry_m, yo(dy), True).wait_recv()
+        for dy in YS + (0,):
+            y_copy(d, r, 2, dy, True).wait_recv()
+        for dy in YS:
+            y_copy(d, r, 0, dy, True).wait_recv()
         for dz in ZR[r]:
             go(z_copy(d, dz, False))
         if r == 0:
@@ -232,11 +229,9 @@
     go(core_copy(1, 2))
     t_step(1, 1)
     g_step(0, 0)
-    h_step(0, 0)
     up(1, 3)
     go(core_copy(1, 3))
     g_step(0, 1)
-    h_step(0, 1)
     f_step(1, 0)
 
     lane = lax.broadcasted_iota(jnp.int32, (128, 128), 1)
@@ -255,9 +250,7 @@
     cp_list.start()
     z_send(0, 1)
     g_step(1, 0)
-    h_step(1, 0)
     g_step(1, 1)
-    h_step(1, 1)
     cp_list.wait()
     for dz in ZS:
         idx_copy(dz, True).wait_recv()
@@ -303,55 +296,40 @@
                 go(zb_copy(d, dz, False))
         qz[d, 0, :, lax.div(z, 2)] = lo[d, z]
 
-    def yb_copy(d, r, kind, yy, arrive):
-        yf = yy if arrive else y
-        p = yy * 2 + (xh if kind == 0 else 1 - xh)
-        dst = plo.at[r, yf, x, c * 2 + d] if kind == 0 else fd.at[d, r, yf]
-        return rc(qz.at[d, r, p], dst, ybs.at[d, r, kind, yy], ybr.at[d, r, kind, yf], dev_y(yy))
+    NS = (3, 2, 1, 0)
+
+    def yb_copy(d, r, n, dy, arrive):
+        yy = yo(dy)
+        yf, xs_ = (yy, rel[n]) if arrive else (y, x)
+        p = yy * 2 + (xh if n < 2 else 1 - xh)
+        return rc(
+            qz.at[d, r, p], plo.at[r, yf, xs_, c * 2 + d],
+            ybs.at[d, r, n, yy], ybr.at[d, r, n, yf], dev_n(n, dy),
+        )
 
     def yb_step(d, r):
         for dz in ZR[r]:
             zb_copy(d, dz, True).wait_recv()
-        for kind in (1, 0):
-            for dy in YS:
-                go(yb_copy(d, r, kind, yo(dy), False))
-        fd[d, r, y] = qz[d, r, y * 2 + 1 - xh]
+        for n in NS:
+            for dy in YS + (0,):
+                if n or dy:
+                    go(yb_copy(d, r, n, dy, False))
         plo[r, y, x, c * 2 + d] = qz[d, r, y * 2 + xh]
 
     def grp(r, xx, cc, d):
         return plo.at[r, :, xx, cc * 2 + d]
 
-    cb_groups = (x, xn, xp, xf)
 
     def cb_copy(d, r, n, cc):
-        ref = grp(r, cb_groups[n], cc, d)
+        ref = grp(r, rel[n], cc, d)
         return rc(ref, ref, cbs.at[d, r, n], cbr.at[d, r, n], dev_core)
 
-    def fb_copy(d, r, xx):
-        return rc(fd.at[d, r], grp(r, xx, c, d), fbs.at[d, r], fbr.at[d, r], dev_xn)
-
-    def xb_copy(d, r, n, src, dst):
-        return rc(grp(r, src, c, d), grp(r, dst, c, d), xbs.at[d, r, n], xbr.at[d, r, n], dev_xp)
-
     def xb_step(d, r):
-        for dy in YS:
-            yb_copy(d, r, 1, yo(dy), True).wait_recv()
-        go(fb_copy(d, r, x))
-        for dy in YS:
-            yb_copy(d, r, 0, yo(dy), True).wait_recv()
-        go(xb_copy(d, r, 0, x, x))
-        go(cb_copy(d, r, 0, c))
-
-    def xb2_step(d, r):
-        fb_copy(d, r, xn).wait_recv()
-        go(xb_copy(d, r, 1, xn, xn))
-        go(cb_copy(d, r, 1, c))
-
-    def xb3_step(d, r):
-        xb_copy(d, r, 0, x, xp).wait_recv()
-        go(cb_copy(d, r, 2, c))
-        xb_copy(d, r, 1, xn, xf).wait_recv()
-        go(cb_copy(d, r, 3, c))
+        for n in NS:
+            for dy in YS + (0,):
+                if n or dy:
+                    yb_copy(d, r, n, dy, True).wait_recv()
+            go(cb_copy(d, r, n, c))
 
     couple(0)
     couple(1)
@@ -360,17 +338,9 @@
     xb_step(0, 0)
     yb_step(1, 0)
     xb_step(0, 1)
-    xb2_step(0, 0)
     yb_step(1, 1)
     xb_step(1, 0)
-    xb2_step(0, 1)
-    xb3_step(0, 0)
     xb_step(1, 1)
-    xb2_step(1, 0)
-    xb3_step(0, 1)
-    xb2_step(1, 1)
-    xb3_step(1, 0)
-    xb3_step(1, 1)
     for d in range(2):
         for r in range(2):
             for n in range(4):
@@ -430,13 +400,11 @@
             blk(2, 2, 2, 4),
             blk(2, 2, 4),
             blk(2, 2, 4),
-            blk(2, 2, 4),
             blk(2, 2, 8),
             pltpu.VMEM((2, 8, 8, 16, 128), BF),
             pltpu.VMEM((ZERO_SLOT + 1, 16, 128), F32),
             pltpu.VMEM((2, 8, 8, 16, 128), BF),
             blk(2, 2, 8),
-            blk(2, 2, 4),
             blk(2, 4, 4, 4),
             pltpu.VMEM((16, 128), jnp.int32),
             pltpu.VMEM((8, 16, 128), jnp.int32),
@@ -446,14 +414,11 @@
             dma((6,)), dma((2,)),
             dma((2, 4)), dma((2, 4)),
             dma((2, 2, 2)), dma((2, 2, 2)),
-            dma((2, 2)), dma((2, 2)),
             dma((2, 2, 2, 4)), dma((2, 2, 2, 4)),
             dma((2, 8)), dma((2, 8)),
             dma((8,)), dma((8,)),
             dma((2, 8)), dma((2, 8)),
-            dma((2, 2, 2, 4)), dma((2, 2, 2, 4)),
-            dma((2, 2)), dma((2, 2)),
-            dma((2, 2, 2)), dma((2, 2, 2)),
+            dma((2, 2, 4, 4)), dma((2, 2, 4, 4)),
             dma((2, 2, 4)), dma((2, 2, 4)),
         ],
         compiler_params=pltpu.CompilerParams(

time: 68.6 us -> 64.6 us (0.942)
  Pallas kernels: 67.5 us -> 63.5 us
    pallas_call x1, Pallas kernels: 67.5 us -> 63.5 us  [body(): pl.pallas_call(kernel, out_shape=pltpu.VMEM((2, 16, 128, 128), BF), in_sp...]
where the time goes in v4:
time: 64.6 us; the launch traced here: 64.5 us
  Pallas kernels  63.5 us (98%)
  local copies, waits for them, and re-layouts  0.97 us (2%)
    pallas_call x1, Pallas kernels, body(): pl.pallas_call(kernel, out_shape=pltpu.VMEM((2, 16, 128, 128), BF), in_sp...  63.5 us

profile of v4, /device:TPU:1, one launch (start us, length us, event | category | flops | bytes accessed | tf_op | source)
XLA Modules:
  0.0 64.5 jit_solution(3830116028459250131)
XLA Ops:
  0.0 63.5 %h2_pass.1 = bf16[2,16,128,128]{3,2,1,0:T(8,128)(2,1)S(1)} custom-call(s32[2,64]{1,0:T(2,128)} %dir_v.1, s32[2,64]{1,0:T(2,128)} %dir_v.1, s32[7,2,8]{2,1,0:T(2,128)} %bitcast.5, s32[7,2,8]{2,1,0:T(2,128)} %bitcast.6, s32[2,8]{1,0:T(2,128)} %bitcast.7, bf16[2,16,128,128]{3,2,1,0:T(8,128)(2,1)} %coef_hbm.1, bf16[2,8,2,128,128]{4,3,2,1,0:T(8,128)(2,1)} %table_hbm.1, ...), custom_call_target="tpu_custom_call" | custom-call | tf_op jit(solution)/shard_map/h2_pass/pallas_call | solution.py:387
  63.5 1.0 %copy.9 = bf16[2,16,128,128]{3,2,1,0:T(8,128)(2,1)} copy(bf16[2,16,128,128]{3,2,1,0:T(8,128)(2,1)S(1)} %h2_pass.1) | data formatting | bytes 2097152

commit v5 on v4

--- a/solution.py
+++ b/solution.py
@@ -70,6 +70,11 @@
     def go(cp):
         cp.start()
         pend.append(cp)
+
+    def drain():
+        for cp in pend:
+            cp.wait_send()
+        pend.clear()
 
     YS = (2, 1, 3)
     ZE = (4, 2, 6)
@@ -340,11 +345,14 @@
     xb_step(0, 1)
     yb_step(1, 1)
     xb_step(1, 0)
+    drain()
     xb_step(1, 1)
     for d in range(2):
         for r in range(2):
             for n in range(4):
                 cb_copy(d, r, n, oc).wait_recv()
+
+    drain()
 
     def down(n, carry):
         cc = lax.div(n, 16)
@@ -368,9 +376,7 @@
         out[cc, i] = t.T.astype(BF)
         return carry
 
-    lax.fori_loop(0, 32, down, 0, unroll=4)
-    for cp in pend:
-        cp.wait_send()
+    lax.fori_loop(0, 32, down, 0, unroll=8)
 
 
 def body(child_coef, transfer, child_dir, couple_src, couple_kind, couple_count, couple_table):

time: 64.6 us -> 63.4 us (0.981)
  Pallas kernels: 63.5 us -> 62.3 us
    pallas_call x1, Pallas kernels: 63.5 us -> 62.3 us  [body(): pl.pallas_call(kernel, out_shape=pltpu.VMEM((2, 16, 128, 128), BF), in_sp...]
where the time goes in v5:
time: 63.4 us; the launch traced here: 63.3 us
  Pallas kernels  62.3 us (98%)
  local copies, waits for them, and re-layouts  0.97 us (2%)
    pallas_call x1, Pallas kernels, body(): pl.pallas_call(kernel, out_shape=pltpu.VMEM((2, 16, 128, 128), BF), in_sp...  62.3 us

profile of v5, /device:TPU:1, one launch (start us, length us, event | category | flops | bytes accessed | tf_op | source)
XLA Modules:
  0.0 63.3 jit_solution(8287329087338995015)
XLA Ops:
  0.0 62.3 %h2_pass.1 = bf16[2,16,128,128]{3,2,1,0:T(8,128)(2,1)S(1)} custom-call(s32[2,64]{1,0:T(2,128)} %dir_v.1, s32[2,64]{1,0:T(2,128)} %dir_v.1, s32[7,2,8]{2,1,0:T(2,128)} %bitcast.5, s32[7,2,8]{2,1,0:T(2,128)} %bitcast.6, s32[2,8]{1,0:T(2,128)} %bitcast.7, bf16[2,16,128,128]{3,2,1,0:T(8,128)(2,1)} %coef_hbm.1, bf16[2,8,2,128,128]{4,3,2,1,0:T(8,128)(2,1)} %table_hbm.1, ...), custom_call_target="tpu_custom_call" | custom-call | tf_op jit(solution)/shard_map/h2_pass/pallas_call | solution.py:393
  62.3 1.0 %copy.9 = bf16[2,16,128,128]{3,2,1,0:T(8,128)(2,1)} copy(bf16[2,16,128,128]{3,2,1,0:T(8,128)(2,1)S(1)} %h2_pass.1) | data formatting | bytes 2097152

commit v6 on v5

--- a/solution.py
+++ b/solution.py
@@ -163,7 +163,7 @@
         src = fw if n else ry_m
         p = yf * 2 + (1 - xh if n and arrive else xh)
         return rc(
-            src.at[d, r, yy], rz.at[d, r, p], ys.at[d, r, n // 2, yy], yr.at[d, r, n // 2, yf], dev_n(n, dy)
+            src.at[d, r, yy], rz.at[d, r, :, p], ys.at[d, r, n // 2, yy], yr.at[d, r, n // 2, yf], dev_n(n, dy)
         )
 
     def f_step(d, r):
@@ -181,13 +181,13 @@
         ry_m[d, r] = add3(d, r, 1)
         for dy in YS:
             go(y_copy(d, r, 0, dy, False))
-        rz[d, r, y * 2 + xh] = ry_m[d, r, y]
+        rz[d, r, :, y * 2 + xh] = ry_m[d, r, y]
 
     def z_copy(d, dz, arrive):
         zz = zo(dz)
         zf = zz if arrive else z
         return rc(
-            rz.at[d, dz % 2, :, lax.div(zz, 2)], pz.at[d, zf], zs.at[d, zz], zr.at[d, zf], dev_z(zz)
+            rz.at[d, dz % 2, lax.div(zz, 2)], pz.at[d, zf], zs.at[d, zz], zr.at[d, zf], dev_z(zz)
         )
 
     def z_send(d, r):
@@ -198,7 +198,7 @@
         for dz in ZR[r]:
             go(z_copy(d, dz, False))
         if r == 0:
-            pz[d, z] = rz[d, 0, :, lax.div(z, 2)]
+            pz[d, z] = rz[d, 0, lax.div(z, 2)]
 
     def idx_copy(dz, arrive):
         zz = zo(dz)
@@ -270,7 +270,7 @@
         zz = zo(dz)
         zf = zz if arrive else z
         return rc(
-            lo.at[d, zz], qz.at[d, dz % 2, :, lax.div(zf, 2)], zbs.at[d, zz], zbr.at[d, zf], dev_z(zz)
+            lo.at[d, zz], qz.at[d, dz % 2, lax.div(zf, 2)], zbs.at[d, zz], zbr.at[d, zf], dev_z(zz)
         )
 
     def couple(d):
@@ -299,7 +299,7 @@
             lax.fori_loop(0, 8, row_sum, 0, unroll=4)
             if dz:
                 go(zb_copy(d, dz, False))
-        qz[d, 0, :, lax.div(z, 2)] = lo[d, z]
+        qz[d, 0, lax.div(z, 2)] = lo[d, z]
 
     NS = (3, 2, 1, 0)
 
@@ -308,7 +308,7 @@
         yf, xs_ = (yy, rel[n]) if arrive else (y, x)
         p = yy * 2 + (xh if n < 2 else 1 - xh)
         return rc(
-            qz.at[d, r, p], plo.at[r, yf, xs_, c * 2 + d],
+            qz.at[d, r, :, p], plo.at[r, yf, xs_, c * 2 + d],
             ybs.at[d, r, n, yy], ybr.at[d, r, n, yf], dev_n(n, dy),
         )
 
@@ -319,7 +319,7 @@
             for dy in YS + (0,):
                 if n or dy:
                     go(yb_copy(d, r, n, dy, False))
-        plo[r, y, x, c * 2 + d] = qz[d, r, y * 2 + xh]
+        plo[r, y, x, c * 2 + d] = qz[d, r, :, y * 2 + xh]
 
     def grp(r, xx, cc, d):
         return plo.at[r, :, xx, cc * 2 + d]
@@ -330,7 +330,7 @@
         return rc(ref, ref, cbs.at[d, r, n], cbr.at[d, r, n], dev_core)
 
     def xb_step(d, r):
-        for n in NS:
+        for n in (0, 1, 2, 3):
             for dy in YS + (0,):
                 if n or dy:
                     yb_copy(d, r, n, dy, True).wait_recv()
@@ -406,11 +406,11 @@
             blk(2, 2, 2, 4),
             blk(2, 2, 4),
             blk(2, 2, 4),
-            blk(2, 2, 8),
+            pltpu.VMEM((2, 2, 4, 8, 16, 128), BF),
             pltpu.VMEM((2, 8, 8, 16, 128), BF),
             pltpu.VMEM((ZERO_SLOT + 1, 16, 128), F32),
             pltpu.VMEM((2, 8, 8, 16, 128), BF),
-            blk(2, 2, 8),
+            pltpu.VMEM((2, 2, 4, 8, 16, 128), BF),
             blk(2, 4, 4, 4),
             pltpu.VMEM((16, 128), jnp.int32),
             pltpu.VMEM((8, 16, 128), jnp.int32),

time: 63.4 us -> 63.4 us (level)
  no operation moved by 1% of the time
where the time goes in v6:
time: 63.4 us; the launch traced here: 63.3 us
  Pallas kernels  62.3 us (98%)
  local copies, waits for them, and re-layouts  0.97 us (2%)
    pallas_call x1, Pallas kernels, body(): pl.pallas_call(kernel, out_shape=pltpu.VMEM((2, 16, 128, 128), BF), in_sp...  62.3 us

profile of v6, /device:TPU:1, one launch (start us, length us, event | category | flops | bytes accessed | tf_op | source)
XLA Modules:
  0.0 63.3 jit_solution(15618175291912868697)
XLA Ops:
  0.0 62.3 %h2_pass.1 = bf16[2,16,128,128]{3,2,1,0:T(8,128)(2,1)S(1)} custom-call(s32[2,64]{1,0:T(2,128)} %dir_v.1, s32[2,64]{1,0:T(2,128)} %dir_v.1, s32[7,2,8]{2,1,0:T(2,128)} %bitcast.5, s32[7,2,8]{2,1,0:T(2,128)} %bitcast.6, s32[2,8]{1,0:T(2,128)} %bitcast.7, bf16[2,16,128,128]{3,2,1,0:T(8,128)(2,1)} %coef_hbm.1, bf16[2,8,2,128,128]{4,3,2,1,0:T(8,128)(2,1)} %table_hbm.1, ...), custom_call_target="tpu_custom_call" | custom-call | tf_op jit(solution)/shard_map/h2_pass/pallas_call | solution.py:393
  62.3 1.0 %copy.9 = bf16[2,16,128,128]{3,2,1,0:T(8,128)(2,1)} copy(bf16[2,16,128,128]{3,2,1,0:T(8,128)(2,1)S(1)} %h2_pass.1) | data formatting | bytes 2097152
